TPU v7x, 128 devices: a whole 4x4x4 slice. The times are simulated.
128 devices in a mesh: dp: 8 (over z_lo, y), pipe: 16 (over z_hi, x, core).
Axes of the slice: x: 4, y: 4, z: 4 (z_hi: 2, z_lo: 2; z = z_hi * 2 + z_lo), core: 2. Of those that a mesh axis runs over, the one named last changes fastest.
Arguments:
- activations: bfloat16 [16, 4096, 8192], P('pipe', 'dp'), may hold values from -6 to 6
- cotangent: bfloat16 [4096, 8192], P('dp'), may hold values from -6 to 6
- adapter_down: bfloat16 [16, 8192, 512], P('pipe'), may hold values from -0.0625 to 0.0625
- adapter_expand: bfloat16 [16, 512, 8192], P('pipe'), may hold values from -0.25 to 0.25
- value_rows: bfloat16 [16, 32, 8192], P('pipe', 'dp'), may hold values from -0.0625 to 0.0625
- input_rows: bfloat16 [16, 32, 8192], P('pipe', 'dp'), may hold values from -0.0625 to 0.0625
- hidden_cols: bfloat16 [16, 32, 512], P('pipe'), may hold values from -0.25 to 0.25
- inner_cols: bfloat16 [16, 32, 512], P('pipe'), may hold values from -0.25 to 0.25
- lengths: int32 [32], P('dp'), may hold values from 1 to 128, as said below
- query_example: int32 [32], replicated, may hold values from 0 to 31
Outputs:
- scores: float32 [32, 32], P('dp')
Inputs may be any that keep to these rules, and one draw needn't show every extreme that they name: `lengths`: live tokens of each example; the rest of its 128 positions is padding.
All inputs are finite; a program needn't handle non-finite values.
Results may differ from a plain program's by a relative error of at most 0.022.
Values may be sent and summed in bfloat16 or wider, within the bound.
A program may use at most 128 MiB of HBM per device.

v0:
```python
import jax
import jax.numpy as jnp
from jax import lax
from jax.sharding import PartitionSpec as P

SLOT = 128


adapter_scale = 0.25


def from_behind(value, axis, steps):
    count = lax.axis_size(axis)
    first, last = (max(0, -steps), min(count, count - steps))
    return lax.ppermute(value, axis, [(source, source + steps) for source in range(first, last)])


def local(
    activations,
    cotangent,
    adapter_down,
    adapter_expand,
    value_rows,
    input_rows,
    hidden_cols,
    inner_cols,
    lengths,
    query_example,
):
    section_total = lax.axis_size("pipe")
    section_index = lax.axis_index("pipe")
    tok_dev = activations.shape[1]
    ex_dev = tok_dev // SLOT
    query_total = hidden_cols.shape[1]
    value_all, input_all = (
        lax.all_gather(value_rows[0], "dp", axis=0, tiled=True),
        lax.all_gather(input_rows[0], "dp", axis=0, tiled=True),
    )
    down_map = adapter_down[0]
    up_map = adapter_expand[0]
    hid_factor = hidden_cols[0]
    inn_factor = inner_cols[0]
    act_local = activations[0]
    block_rows = SLOT
    block_count = tok_dev // block_rows
    step_count = block_count + section_total - 1
    is_last = section_index == section_total - 1

    def advance(step_index, carry):
        incoming, per_token = carry
        block_index = step_index - (section_total - 1 - section_index)
        is_valid = (block_index >= 0) & (block_index < block_count)
        row_start = jnp.clip(block_index, 0, block_count - 1) * block_rows
        seed_rows = lax.dynamic_slice_in_dim(cotangent, row_start, block_rows, 0)
        gradient_leaving = jnp.where(is_last, seed_rows, incoming)

        def compute(unused):
            act_rows = lax.dynamic_slice_in_dim(act_local, row_start, block_rows, 0)
            hidden = jnp.dot(act_rows, down_map, preferred_element_type=jnp.float32).astype(
                jnp.bfloat16
            )
            inner_gradient = (
                adapter_scale
                * jnp.einsum(
                    "td,rd->tr", gradient_leaving, up_map, preferred_element_type=jnp.float32
                )
            ).astype(jnp.bfloat16)
            gradient_entering = (
                gradient_leaving.astype(jnp.float32)
                + jnp.einsum(
                    "tr,dr->td", inner_gradient, down_map, preferred_element_type=jnp.float32
                )
            ).astype(jnp.bfloat16)
            hidden_projection = jnp.einsum(
                "tr,qr->tq", hidden, hid_factor, preferred_element_type=jnp.float32
            )
            value_projection = jnp.einsum(
                "td,qd->tq", gradient_leaving, value_all, preferred_element_type=jnp.float32
            )
            input_projection = jnp.einsum(
                "td,qd->tq", act_rows, input_all, preferred_element_type=jnp.float32
            )
            inner_projection = jnp.einsum(
                "tr,qr->tq", inner_gradient, inn_factor, preferred_element_type=jnp.float32
            )
            return (
                gradient_entering,
                adapter_scale * hidden_projection * value_projection
                + input_projection * inner_projection,
            )

        def skipped(unused):
            return (
                jnp.zeros_like(gradient_leaving),
                jnp.zeros((block_rows, query_total), jnp.float32),
            )

        gradient_entering, summand_rows = lax.cond(is_valid, compute, skipped, 0)
        previous = lax.dynamic_slice_in_dim(per_token, row_start, block_rows, 0)
        per_token = lax.dynamic_update_slice_in_dim(
            per_token, previous + summand_rows, row_start, 0
        )
        incoming = from_behind(gradient_entering, "pipe", -1)
        return (incoming, per_token)

    start_grad = jnp.zeros((block_rows, act_local.shape[1]), jnp.bfloat16)
    start_terms = jnp.zeros((tok_dev, query_total), jnp.float32)
    final_grad, per_token = lax.fori_loop(0, step_count, advance, (start_grad, start_terms))
    offsets = lax.broadcasted_iota(jnp.int32, (tok_dev,), 0) % SLOT
    live_mask = (offsets < jnp.repeat(lengths, SLOT, total_repeat_length=tok_dev)).astype(
        jnp.float32
    )
    masked = per_token * live_mask[:, None]
    local_sums = jnp.sum(masked.reshape(ex_dev, SLOT, query_total), axis=1)
    totals = lax.psum(local_sums, "pipe") * SLOT ** (-0.5)
    example_ids = lax.axis_index("dp") * ex_dev + lax.broadcasted_iota(jnp.int32, (ex_dev,), 0)
    keep_mask = (example_ids[:, None] != query_example[None, :]).astype(jnp.float32)
    return totals * keep_mask


def solution(mesh):
    in_specs = (
        P("pipe", "dp", None),
        P("dp", None),
        P("pipe", None, None),
        P("pipe", None, None),
        P("pipe", "dp", None),
        P("pipe", "dp", None),
        P("pipe", None, None),
        P("pipe", None, None),
        P("dp"),
        P(),
    )
    out_specs = P("dp", None)
    return jax.shard_map(local, mesh=mesh, in_specs=in_specs, out_specs=out_specs, check_vma=False)
```

profile of v0, /device:TPU:1, one launch (start us, length us, event | category | flops | bytes accessed | tf_op | source)
XLA Modules:
  0.0 908.4 jit_solution(10851682348993537943)
XLA Ops:
  1.0 26.8 %all-gather = bf16[1,32,8192]{2,0,1:T(2,128)(2,1)S(1)} all-gather(bf16[1,4,8192]{2,0,1:T(2,128)(2,1)S(1)} %copy.14), channel_id=2, replica_groups=mesh['dp'=8,'pipe'=16] {'dp'}, dimensions={1}, use_global_device_ids=true | all-gather | bytes 589824 | tf_op jit(solution)/shard_map/all_gather | solution.py:36
  28.5 25.3 %all-gather.1 = bf16[1,32,8192]{2,0,1:T(2,128)(2,1)S(1)} all-gather(bf16[1,4,8192]{2,0,1:T(2,128)(2,1)S(1)} %copy.15), channel_id=3, replica_groups=mesh['dp'=8,'pipe'=16] {'dp'}, dimensions={1}, use_global_device_ids=true | all-gather | bytes 589824 | tf_op jit(solution)/shard_map/all_gather | solution.py:37
  54.7 790.2 %while.18 = (s32[]{:T(128)}, bf16[128,8192]{1,0:T(8,128)(2,1)S(1)}, f32[512,32]{0,1:T(8,128)S(1)}, s32[]{:T(128)}, pred[]{:T(512)}, /*index=5*/bf16[512,8192]{1,...) while((s32[]{:T(128)}, bf16[128,8192]{1,0:T(8,128)(2,1)S(1)}, ...), condition=%wide.region_3.4_spmd, body=%wide.region_0.3_spmd.sunk | while | flops 3368243200 | bytes 79266320 | solution.py:108
  56.3 12.4 %collective-permute-start = (bf16[128,8192]{1,0:T(8,128)(2,1)}, bf16[128,8192]{1,0:T(8,128)(2,1)S(1)}, u32[]{:S(2)}, u32[]{:S(2)}) collective-permute-start(bf16[128,8192]{1,0:T(8,128)(2,1)} %get-tuple-element.491), channel_id=1, source_target_pairs={{1,0},{2,1},{3,2},{4,3},{5,4},{6,5},{7,6},{8,7},{9,8},{10,9},{11,1... | collective-permute-start | bytes 6291464 | tf_op jit(solution)/shard_map/while/body/eval_jaxpr/ppermute | solution.py:15
  68.6 25.0 %collective-permute-done = bf16[128,8192]{1,0:T(8,128)(2,1)S(1)} collective-permute-done((bf16[128,8192]{1,0:T(8,128)(2,1)}, bf16[128,8192]{1,0:T(8,128)(2,1)S(1)}, u32[]{:S(2)}, u32[]{:S(2)}) %collective-permute-start) | collective-permute-done | bytes 2097184 | tf_op jit(solution)/shard_map/while/body/eval_jaxpr/ppermute | solution.py:15
  97.1 25.6 %collective-permute-done = bf16[128,8192]{1,0:T(8,128)(2,1)S(1)} collective-permute-done((bf16[128,8192]{1,0:T(8,128)(2,1)}, bf16[128,8192]{1,0:T(8,128)(2,1)S(1)}, u32[]{:S(2)}, u32[]{:S(2)}) %collective-permute-start) | collective-permute-done | bytes 2097184 | tf_op jit(solution)/shard_map/while/body/eval_jaxpr/ppermute | solution.py:15
  126.2 25.6 %collective-permute-done = bf16[128,8192]{1,0:T(8,128)(2,1)S(1)} collective-permute-done((bf16[128,8192]{1,0:T(8,128)(2,1)}, bf16[128,8192]{1,0:T(8,128)(2,1)S(1)}, u32[]{:S(2)}, u32[]{:S(2)}) %collective-permute-start) | collective-permute-done | bytes 2097184 | tf_op jit(solution)/shard_map/while/body/eval_jaxpr/ppermute | solution.py:15
  155.3 25.6 %collective-permute-done = bf16[128,8192]{1,0:T(8,128)(2,1)S(1)} collective-permute-done((bf16[128,8192]{1,0:T(8,128)(2,1)}, bf16[128,8192]{1,0:T(8,128)(2,1)S(1)}, u32[]{:S(2)}, u32[]{:S(2)}) %collective-permute-start) | collective-permute-done | bytes 2097184 | tf_op jit(solution)/shard_map/while/body/eval_jaxpr/ppermute | solution.py:15
  184.4 25.6 %collective-permute-done = bf16[128,8192]{1,0:T(8,128)(2,1)S(1)} collective-permute-done((bf16[128,8192]{1,0:T(8,128)(2,1)}, bf16[128,8192]{1,0:T(8,128)(2,1)S(1)}, u32[]{:S(2)}, u32[]{:S(2)}) %collective-permute-start) | collective-permute-done | bytes 2097184 | tf_op jit(solution)/shard_map/while/body/eval_jaxpr/ppermute | solution.py:15
  213.5 25.6 %collective-permute-done = bf16[128,8192]{1,0:T(8,128)(2,1)S(1)} collective-permute-done((bf16[128,8192]{1,0:T(8,128)(2,1)}, bf16[128,8192]{1,0:T(8,128)(2,1)S(1)}, u32[]{:S(2)}, u32[]{:S(2)}) %collective-permute-start) | collective-permute-done | bytes 2097184 | tf_op jit(solution)/shard_map/while/body/eval_jaxpr/ppermute | solution.py:15
  242.6 25.6 %collective-permute-done = bf16[128,8192]{1,0:T(8,128)(2,1)S(1)} collective-permute-done((bf16[128,8192]{1,0:T(8,128)(2,1)}, bf16[128,8192]{1,0:T(8,128)(2,1)S(1)}, u32[]{:S(2)}, u32[]{:S(2)}) %collective-permute-start) | collective-permute-done | bytes 2097184 | tf_op jit(solution)/shard_map/while/body/eval_jaxpr/ppermute | solution.py:15
  271.7 25.6 %collective-permute-done = bf16[128,8192]{1,0:T(8,128)(2,1)S(1)} collective-permute-done((bf16[128,8192]{1,0:T(8,128)(2,1)}, bf16[128,8192]{1,0:T(8,128)(2,1)S(1)}, u32[]{:S(2)}, u32[]{:S(2)}) %collective-permute-start) | collective-permute-done | bytes 2097184 | tf_op jit(solution)/shard_map/while/body/eval_jaxpr/ppermute | solution.py:15
  300.9 25.6 %collective-permute-done = bf16[128,8192]{1,0:T(8,128)(2,1)S(1)} collective-permute-done((bf16[128,8192]{1,0:T(8,128)(2,1)}, bf16[128,8192]{1,0:T(8,128)(2,1)S(1)}, u32[]{:S(2)}, u32[]{:S(2)}) %collective-permute-start) | collective-permute-done | bytes 2097184 | tf_op jit(solution)/shard_map/while/body/eval_jaxpr/ppermute | solution.py:15
  330.0 25.6 %collective-permute-done = bf16[128,8192]{1,0:T(8,128)(2,1)S(1)} collective-permute-done((bf16[128,8192]{1,0:T(8,128)(2,1)}, bf16[128,8192]{1,0:T(8,128)(2,1)S(1)}, u32[]{:S(2)}, u32[]{:S(2)}) %collective-permute-start) | collective-permute-done | bytes 2097184 | tf_op jit(solution)/shard_map/while/body/eval_jaxpr/ppermute | solution.py:15
  359.1 25.6 %collective-permute-done = bf16[128,8192]{1,0:T(8,128)(2,1)S(1)} collective-permute-done((bf16[128,8192]{1,0:T(8,128)(2,1)}, bf16[128,8192]{1,0:T(8,128)(2,1)S(1)}, u32[]{:S(2)}, u32[]{:S(2)}) %collective-permute-start) | collective-permute-done | bytes 2097184 | tf_op jit(solution)/shard_map/while/body/eval_jaxpr/ppermute | solution.py:15
  388.2 25.6 %collective-permute-done = bf16[128,8192]{1,0:T(8,128)(2,1)S(1)} collective-permute-done((bf16[128,8192]{1,0:T(8,128)(2,1)}, bf16[128,8192]{1,0:T(8,128)(2,1)S(1)}, u32[]{:S(2)}, u32[]{:S(2)}) %collective-permute-start) | collective-permute-done | bytes 2097184 | tf_op jit(solution)/shard_map/while/body/eval_jaxpr/ppermute | solution.py:15
  417.3 25.6 %collective-permute-done = bf16[128,8192]{1,0:T(8,128)(2,1)S(1)} collective-permute-done((bf16[128,8192]{1,0:T(8,128)(2,1)}, bf16[128,8192]{1,0:T(8,128)(2,1)S(1)}, u32[]{:S(2)}, u32[]{:S(2)}) %collective-permute-start) | collective-permute-done | bytes 2097184 | tf_op jit(solution)/shard_map/while/body/eval_jaxpr/ppermute | solution.py:15
  446.4 160.8 %collective-permute-done = bf16[128,8192]{1,0:T(8,128)(2,1)S(1)} collective-permute-done((bf16[128,8192]{1,0:T(8,128)(2,1)}, bf16[128,8192]{1,0:T(8,128)(2,1)S(1)}, u32[]{:S(2)}, u32[]{:S(2)}) %collective-permute-start) | collective-permute-done | bytes 2097184 | tf_op jit(solution)/shard_map/while/body/eval_jaxpr/ppermute | solution.py:15
  607.1 22.1 %conditional.2 = (bf16[128,8192]{1,0:T(8,128)(2,1)}, f32[128,32]{0,1:T(8,128)S(1)}) conditional(s32[]{:T(128)} %convert_element_type.46, () %tuple.54, (pred[]{:T(512)}, bf16[512,8192]{1,0:T(8,128)(2,1)}, s32[]{:T(128)}, bf16[128,8192]{1,0:T(8,128)(2,1)S(1)}, bf16[512,8192]{1,0:T(8,128)(2,1)}, /*index=5*/bf16[8192,512]{1,0:T(8,128)(2,1)}, s32[]{:T(128)}, ...), branch_computations={%region_1.1_spmd, %region_2.2_spmd} | conditional | flops 3368239104 | bytes 70828144 | solution.py:98
  609.7 6.5 fusion.5
  631.2 29.2 %collective-permute-done = bf16[128,8192]{1,0:T(8,128)(2,1)S(1)} collective-permute-done((bf16[128,8192]{1,0:T(8,128)(2,1)}, bf16[128,8192]{1,0:T(8,128)(2,1)S(1)}, u32[]{:S(2)}, u32[]{:S(2)}) %collective-permute-start) | collective-permute-done | bytes 2097184 | tf_op jit(solution)/shard_map/while/body/eval_jaxpr/ppermute | solution.py:15
  660.4 22.1 %conditional.2 = (bf16[128,8192]{1,0:T(8,128)(2,1)}, f32[128,32]{0,1:T(8,128)S(1)}) conditional(s32[]{:T(128)} %convert_element_type.46, () %tuple.54, (pred[]{:T(512)}, bf16[512,8192]{1,0:T(8,128)(2,1)}, s32[]{:T(128)}, bf16[128,8192]{1,0:T(8,128)(2,1)S(1)}, bf16[512,8192]{1,0:T(8,128)(2,1)}, /*index=5*/bf16[8192,512]{1,0:T(8,128)(2,1)}, s32[]{:T(128)}, ...), branch_computations={%region_1.1_spmd, %region_2.2_spmd} | conditional | flops 3368239104 | bytes 70828144 | solution.py:98
  663.0 6.5 fusion.5
  684.4 29.2 %collective-permute-done = bf16[128,8192]{1,0:T(8,128)(2,1)S(1)} collective-permute-done((bf16[128,8192]{1,0:T(8,128)(2,1)}, bf16[128,8192]{1,0:T(8,128)(2,1)S(1)}, u32[]{:S(2)}, u32[]{:S(2)}) %collective-permute-start) | collective-permute-done | bytes 2097184 | tf_op jit(solution)/shard_map/while/body/eval_jaxpr/ppermute | solution.py:15
  713.7 22.1 %conditional.2 = (bf16[128,8192]{1,0:T(8,128)(2,1)}, f32[128,32]{0,1:T(8,128)S(1)}) conditional(s32[]{:T(128)} %convert_element_type.46, () %tuple.54, (pred[]{:T(512)}, bf16[512,8192]{1,0:T(8,128)(2,1)}, s32[]{:T(128)}, bf16[128,8192]{1,0:T(8,128)(2,1)S(1)}, bf16[512,8192]{1,0:T(8,128)(2,1)}, /*index=5*/bf16[8192,512]{1,0:T(8,128)(2,1)}, s32[]{:T(128)}, ...), branch_computations={%region_1.1_spmd, %region_2.2_spmd} | conditional | flops 3368239104 | bytes 70828144 | solution.py:98
  716.2 6.5 fusion.5
  737.7 28.5 %collective-permute-done = bf16[128,8192]{1,0:T(8,128)(2,1)S(1)} collective-permute-done((bf16[128,8192]{1,0:T(8,128)(2,1)}, bf16[128,8192]{1,0:T(8,128)(2,1)S(1)}, u32[]{:S(2)}, u32[]{:S(2)}) %collective-permute-start) | collective-permute-done | bytes 2097184 | tf_op jit(solution)/shard_map/while/body/eval_jaxpr/ppermute | solution.py:15
  766.2 22.0 %conditional.2 = (bf16[128,8192]{1,0:T(8,128)(2,1)}, f32[128,32]{0,1:T(8,128)S(1)}) conditional(s32[]{:T(128)} %convert_element_type.46, () %tuple.54, (pred[]{:T(512)}, bf16[512,8192]{1,0:T(8,128)(2,1)}, s32[]{:T(128)}, bf16[128,8192]{1,0:T(8,128)(2,1)S(1)}, bf16[512,8192]{1,0:T(8,128)(2,1)}, /*index=5*/bf16[8192,512]{1,0:T(8,128)(2,1)}, s32[]{:T(128)}, ...), branch_computations={%region_1.1_spmd, %region_2.2_spmd} | conditional | flops 3368239104 | bytes 70828144 | solution.py:98
  768.7 6.5 fusion.5
  790.1 25.6 %collective-permute-done = bf16[128,8192]{1,0:T(8,128)(2,1)S(1)} collective-permute-done((bf16[128,8192]{1,0:T(8,128)(2,1)}, bf16[128,8192]{1,0:T(8,128)(2,1)S(1)}, u32[]{:S(2)}, u32[]{:S(2)}) %collective-permute-start) | collective-permute-done | bytes 2097184 | tf_op jit(solution)/shard_map/while/body/eval_jaxpr/ppermute | solution.py:15
  819.2 25.6 %collective-permute-done = bf16[128,8192]{1,0:T(8,128)(2,1)S(1)} collective-permute-done((bf16[128,8192]{1,0:T(8,128)(2,1)}, bf16[128,8192]{1,0:T(8,128)(2,1)S(1)}, u32[]{:S(2)}, u32[]{:S(2)}) %collective-permute-start) | collective-permute-done | bytes 2097184 | tf_op jit(solution)/shard_map/while/body/eval_jaxpr/ppermute | solution.py:15
  848.3 59.4 %psum.7 = f32[4,32]{0,1:T(8,128)S(1)} all-reduce(f32[4,32]{0,1:T(8,128)S(1)} %reduce_sum.9), channel_id=1, replica_groups=mesh['dp'=8,'pipe'=16] {'pipe'}, use_global_device_ids=true, to_apply=%region_5.6 | all-reduce | flops 128 | bytes 1024 | tf_op jit(solution)/shard_map/psum | solution.py:115
  (153 shorter events, 149.9 us)
Async XLA Ops:
  0.0 28.4 %copy-start.2 = (bf16[1,4,8192]{2,1,0:T(4,128)(2,1)S(1)}, bf16[1,4,8192]{2,1,0:T(4,128)(2,1)}, u32[]{:S(2)}) copy-start(bf16[1,4,8192]{2,1,0:T(4,128)(2,1)} %param.21) | copy-start | bytes 196612
  53.8 0.8 copy-start
  53.8 0.8 copy-start.1
  54.6 790.2 %copy-start.3 = (s32[4]{0:T(128)S(1)}, s32[4]{0:T(128)}, u32[]{:S(2)}) copy-start(s32[4]{0:T(128)} %param.24) | copy-start | bytes 52
  54.6 853.0 %copy-start.4 = (s32[32]{0:T(128)S(1)}, s32[32]{0:T(128)}, u32[]{:S(2)}) copy-start(s32[32]{0:T(128)} %param.25) | copy-start | bytes 388
  56.3 37.4 %collective-permute-start = (bf16[128,8192]{1,0:T(8,128)(2,1)}, bf16[128,8192]{1,0:T(8,128)(2,1)S(1)}, u32[]{:S(2)}, u32[]{:S(2)}) collective-permute-start(bf16[128,8192]{1,0:T(8,128)(2,1)} %get-tuple-element.491), channel_id=1, source_target_pairs={{1,0},{2,1},{3,2},{4,3},{5,4},{6,5},{7,6},{8,7},{9,8},{10,9},{11,1... | collective-permute-start | bytes 6291464 | tf_op jit(solution)/shard_map/while/body/eval_jaxpr/ppermute | solution.py:15
  95.2 27.6 %collective-permute-start = (bf16[128,8192]{1,0:T(8,128)(2,1)}, bf16[128,8192]{1,0:T(8,128)(2,1)S(1)}, u32[]{:S(2)}, u32[]{:S(2)}) collective-permute-start(bf16[128,8192]{1,0:T(8,128)(2,1)} %get-tuple-element.491), channel_id=1, source_target_pairs={{1,0},{2,1},{3,2},{4,3},{5,4},{6,5},{7,6},{8,7},{9,8},{10,9},{11,1... | collective-permute-start | bytes 6291464 | tf_op jit(solution)/shard_map/while/body/eval_jaxpr/ppermute | solution.py:15
  124.3 27.6 %collective-permute-start = (bf16[128,8192]{1,0:T(8,128)(2,1)}, bf16[128,8192]{1,0:T(8,128)(2,1)S(1)}, u32[]{:S(2)}, u32[]{:S(2)}) collective-permute-start(bf16[128,8192]{1,0:T(8,128)(2,1)} %get-tuple-element.491), channel_id=1, source_target_pairs={{1,0},{2,1},{3,2},{4,3},{5,4},{6,5},{7,6},{8,7},{9,8},{10,9},{11,1... | collective-permute-start | bytes 6291464 | tf_op jit(solution)/shard_map/while/body/eval_jaxpr/ppermute | solution.py:15
  153.4 27.6 %collective-permute-start = (bf16[128,8192]{1,0:T(8,128)(2,1)}, bf16[128,8192]{1,0:T(8,128)(2,1)S(1)}, u32[]{:S(2)}, u32[]{:S(2)}) collective-permute-start(bf16[128,8192]{1,0:T(8,128)(2,1)} %get-tuple-element.491), channel_id=1, source_target_pairs={{1,0},{2,1},{3,2},{4,3},{5,4},{6,5},{7,6},{8,7},{9,8},{10,9},{11,1... | collective-permute-start | bytes 6291464 | tf_op jit(solution)/shard_map/while/body/eval_jaxpr/ppermute | solution.py:15
  182.5 27.6 %collective-permute-start = (bf16[128,8192]{1,0:T(8,128)(2,1)}, bf16[128,8192]{1,0:T(8,128)(2,1)S(1)}, u32[]{:S(2)}, u32[]{:S(2)}) collective-permute-start(bf16[128,8192]{1,0:T(8,128)(2,1)} %get-tuple-element.491), channel_id=1, source_target_pairs={{1,0},{2,1},{3,2},{4,3},{5,4},{6,5},{7,6},{8,7},{9,8},{10,9},{11,1... | collective-permute-start | bytes 6291464 | tf_op jit(solution)/shard_map/while/body/eval_jaxpr/ppermute | solution.py:15
  211.6 27.6 %collective-permute-start = (bf16[128,8192]{1,0:T(8,128)(2,1)}, bf16[128,8192]{1,0:T(8,128)(2,1)S(1)}, u32[]{:S(2)}, u32[]{:S(2)}) collective-permute-start(bf16[128,8192]{1,0:T(8,128)(2,1)} %get-tuple-element.491), channel_id=1, source_target_pairs={{1,0},{2,1},{3,2},{4,3},{5,4},{6,5},{7,6},{8,7},{9,8},{10,9},{11,1... | collective-permute-start | bytes 6291464 | tf_op jit(solution)/shard_map/while/body/eval_jaxpr/ppermute | solution.py:15
  240.7 27.6 %collective-permute-start = (bf16[128,8192]{1,0:T(8,128)(2,1)}, bf16[128,8192]{1,0:T(8,128)(2,1)S(1)}, u32[]{:S(2)}, u32[]{:S(2)}) collective-permute-start(bf16[128,8192]{1,0:T(8,128)(2,1)} %get-tuple-element.491), channel_id=1, source_target_pairs={{1,0},{2,1},{3,2},{4,3},{5,4},{6,5},{7,6},{8,7},{9,8},{10,9},{11,1... | collective-permute-start | bytes 6291464 | tf_op jit(solution)/shard_map/while/body/eval_jaxpr/ppermute | solution.py:15
  269.8 27.6 %collective-permute-start = (bf16[128,8192]{1,0:T(8,128)(2,1)}, bf16[128,8192]{1,0:T(8,128)(2,1)S(1)}, u32[]{:S(2)}, u32[]{:S(2)}) collective-permute-start(bf16[128,8192]{1,0:T(8,128)(2,1)} %get-tuple-element.491), channel_id=1, source_target_pairs={{1,0},{2,1},{3,2},{4,3},{5,4},{6,5},{7,6},{8,7},{9,8},{10,9},{11,1... | collective-permute-start | bytes 6291464 | tf_op jit(solution)/shard_map/while/body/eval_jaxpr/ppermute | solution.py:15
  298.9 27.6 %collective-permute-start = (bf16[128,8192]{1,0:T(8,128)(2,1)}, bf16[128,8192]{1,0:T(8,128)(2,1)S(1)}, u32[]{:S(2)}, u32[]{:S(2)}) collective-permute-start(bf16[128,8192]{1,0:T(8,128)(2,1)} %get-tuple-element.491), channel_id=1, source_target_pairs={{1,0},{2,1},{3,2},{4,3},{5,4},{6,5},{7,6},{8,7},{9,8},{10,9},{11,1... | collective-permute-start | bytes 6291464 | tf_op jit(solution)/shard_map/while/body/eval_jaxpr/ppermute | solution.py:15
  328.0 27.6 %collective-permute-start = (bf16[128,8192]{1,0:T(8,128)(2,1)}, bf16[128,8192]{1,0:T(8,128)(2,1)S(1)}, u32[]{:S(2)}, u32[]{:S(2)}) collective-permute-start(bf16[128,8192]{1,0:T(8,128)(2,1)} %get-tuple-element.491), channel_id=1, source_target_pairs={{1,0},{2,1},{3,2},{4,3},{5,4},{6,5},{7,6},{8,7},{9,8},{10,9},{11,1... | collective-permute-start | bytes 6291464 | tf_op jit(solution)/shard_map/while/body/eval_jaxpr/ppermute | solution.py:15
  357.1 27.6 %collective-permute-start = (bf16[128,8192]{1,0:T(8,128)(2,1)}, bf16[128,8192]{1,0:T(8,128)(2,1)S(1)}, u32[]{:S(2)}, u32[]{:S(2)}) collective-permute-start(bf16[128,8192]{1,0:T(8,128)(2,1)} %get-tuple-element.491), channel_id=1, source_target_pairs={{1,0},{2,1},{3,2},{4,3},{5,4},{6,5},{7,6},{8,7},{9,8},{10,9},{11,1... | collective-permute-start | bytes 6291464 | tf_op jit(solution)/shard_map/while/body/eval_jaxpr/ppermute | solution.py:15
  386.2 27.6 %collective-permute-start = (bf16[128,8192]{1,0:T(8,128)(2,1)}, bf16[128,8192]{1,0:T(8,128)(2,1)S(1)}, u32[]{:S(2)}, u32[]{:S(2)}) collective-permute-start(bf16[128,8192]{1,0:T(8,128)(2,1)} %get-tuple-element.491), channel_id=1, source_target_pairs={{1,0},{2,1},{3,2},{4,3},{5,4},{6,5},{7,6},{8,7},{9,8},{10,9},{11,1... | collective-permute-start | bytes 6291464 | tf_op jit(solution)/shard_map/while/body/eval_jaxpr/ppermute | solution.py:15
  415.3 27.6 %collective-permute-start = (bf16[128,8192]{1,0:T(8,128)(2,1)}, bf16[128,8192]{1,0:T(8,128)(2,1)S(1)}, u32[]{:S(2)}, u32[]{:S(2)}) collective-permute-start(bf16[128,8192]{1,0:T(8,128)(2,1)} %get-tuple-element.491), channel_id=1, source_target_pairs={{1,0},{2,1},{3,2},{4,3},{5,4},{6,5},{7,6},{8,7},{9,8},{10,9},{11,1... | collective-permute-start | bytes 6291464 | tf_op jit(solution)/shard_map/while/body/eval_jaxpr/ppermute | solution.py:15
  444.4 162.7 %collective-permute-start = (bf16[128,8192]{1,0:T(8,128)(2,1)}, bf16[128,8192]{1,0:T(8,128)(2,1)S(1)}, u32[]{:S(2)}, u32[]{:S(2)}) collective-permute-start(bf16[128,8192]{1,0:T(8,128)(2,1)} %get-tuple-element.491), channel_id=1, source_target_pairs={{1,0},{2,1},{3,2},{4,3},{5,4},{6,5},{7,6},{8,7},{9,8},{10,9},{11,1... | collective-permute-start | bytes 6291464 | tf_op jit(solution)/shard_map/while/body/eval_jaxpr/ppermute | solution.py:15
  607.1 9.0 slice-start
  609.7 6.5 slice-start.1
  629.2 31.2 %collective-permute-start = (bf16[128,8192]{1,0:T(8,128)(2,1)}, bf16[128,8192]{1,0:T(8,128)(2,1)S(1)}, u32[]{:S(2)}, u32[]{:S(2)}) collective-permute-start(bf16[128,8192]{1,0:T(8,128)(2,1)} %get-tuple-element.491), channel_id=1, source_target_pairs={{1,0},{2,1},{3,2},{4,3},{5,4},{6,5},{7,6},{8,7},{9,8},{10,9},{11,1... | collective-permute-start | bytes 6291464 | tf_op jit(solution)/shard_map/while/body/eval_jaxpr/ppermute | solution.py:15
  660.4 9.0 slice-start
  663.0 6.5 slice-start.1
  682.5 31.2 %collective-permute-start = (bf16[128,8192]{1,0:T(8,128)(2,1)}, bf16[128,8192]{1,0:T(8,128)(2,1)S(1)}, u32[]{:S(2)}, u32[]{:S(2)}) collective-permute-start(bf16[128,8192]{1,0:T(8,128)(2,1)} %get-tuple-element.491), channel_id=1, source_target_pairs={{1,0},{2,1},{3,2},{4,3},{5,4},{6,5},{7,6},{8,7},{9,8},{10,9},{11,1... | collective-permute-start | bytes 6291464 | tf_op jit(solution)/shard_map/while/body/eval_jaxpr/ppermute | solution.py:15
  713.7 9.0 slice-start
  716.2 6.5 slice-start.1
  735.7 30.5 %collective-permute-start = (bf16[128,8192]{1,0:T(8,128)(2,1)}, bf16[128,8192]{1,0:T(8,128)(2,1)S(1)}, u32[]{:S(2)}, u32[]{:S(2)}) collective-permute-start(bf16[128,8192]{1,0:T(8,128)(2,1)} %get-tuple-element.491), channel_id=1, source_target_pairs={{1,0},{2,1},{3,2},{4,3},{5,4},{6,5},{7,6},{8,7},{9,8},{10,9},{11,1... | collective-permute-start | bytes 6291464 | tf_op jit(solution)/shard_map/while/body/eval_jaxpr/ppermute | solution.py:15
  766.2 9.0 slice-start
  768.7 6.5 slice-start.1
  788.2 27.6 %collective-permute-start = (bf16[128,8192]{1,0:T(8,128)(2,1)}, bf16[128,8192]{1,0:T(8,128)(2,1)S(1)}, u32[]{:S(2)}, u32[]{:S(2)}) collective-permute-start(bf16[128,8192]{1,0:T(8,128)(2,1)} %get-tuple-element.491), channel_id=1, source_target_pairs={{1,0},{2,1},{3,2},{4,3},{5,4},{6,5},{7,6},{8,7},{9,8},{10,9},{11,1... | collective-permute-start | bytes 6291464 | tf_op jit(solution)/shard_map/while/body/eval_jaxpr/ppermute | solution.py:15
  817.3 27.6 %collective-permute-start = (bf16[128,8192]{1,0:T(8,128)(2,1)}, bf16[128,8192]{1,0:T(8,128)(2,1)S(1)}, u32[]{:S(2)}, u32[]{:S(2)}) collective-permute-start(bf16[128,8192]{1,0:T(8,128)(2,1)} %get-tuple-element.491), channel_id=1, source_target_pairs={{1,0},{2,1},{3,2},{4,3},{5,4},{6,5},{7,6},{8,7},{9,8},{10,9},{11,1... | collective-permute-start | bytes 6291464 | tf_op jit(solution)/shard_map/while/body/eval_jaxpr/ppermute | solution.py:15
where the time goes:
time: 914 us; the launch traced here: 908 us
  waiting for transfers between devices  631 us (69%)
  blocking collectives  111 us (12%)
  matrix products  77.8 us (9%)
  starting transfers between devices  46.8 us (5%)
  local copies, waits for them, and re-layouts  27.1 us (3%)
  other arithmetic  13.2 us (1%)
    ppermute x19, waiting for transfers between devices, from_behind(): lax.ppermute(value, axis, [(source, source + steps) for source in range(f...  631 us
    psum x1, blocking collectives, local(): totals = lax.psum(local_sums, 'pipe') * SLOT ** (-0.5)  59.4 us
    ppermute x19, starting transfers between devices, from_behind(): lax.ppermute(value, axis, [(source, source + steps) for source in range(f...  46.8 us
    all_gather x1, blocking collectives, local(): lax.all_gather(value_rows[0], 'dp', axis=0, tiled=True)  26.8 us
    dot_general x4, matrix products, compute(): jnp.einsum('td,rd->tr', gradient_leaving, up_map, preferred_element_type=...  25.8 us
    all_gather x1, blocking collectives, local(): lax.all_gather(input_rows[0], 'dp', axis=0, tiled=True)  25.3 us
    another operation x31, local copies, waits for them, and re-layouts  23.5 us
    dot_general x4, matrix products, compute(): jnp.einsum('tr,qr->tq', hidden, hid_factor, preferred_element_type=jnp.fl...  21.8 us
  transfers between devices with their start and end apart: 19, of which 19 were waited for; matrix products, arithmetic and copies ran while one was open for 0% of the time, Pallas kernels for 0%

commit v1 on v0

v1 whole, which is shorter than its diff:
```python
import functools

import jax
import jax.numpy as jnp
from jax import lax
from jax.experimental import pallas as pl
from jax.experimental.pallas import tpu as pltpu
from jax.sharding import PartitionSpec as P

SLOT = 128
ADAPTER_SCALE = 0.25
MESH = pl.DeviceIdType.MESH
F32 = jnp.float32
BF16 = jnp.bfloat16
CHUNKS = 4
PIECES = 8
HEAD = 2


def nt(a, b):
    return lax.dot_general(a, b, (((1,), (1,)), ((), ())), preferred_element_type=F32)


def kernel(
    n_dp,
    n_pipe,
    x_hbm,
    cot_hbm,
    d_hbm,
    e_hbm,
    v_ref,
    i_ref,
    hc_ref,
    ic_ref,
    len_ref,
    qe_ref,
    out_ref,
    x_v,
    cot_v,
    d_v,
    e_v,
    z_in,
    z_out,
    a_all,
    hp_all,
    rows_all,
    u_acc,
    u_bf,
    own_acc,
    hp_acc,
    total,
    s_all,
    load_e,
    load_d,
    load_cot,
    load_x,
    rows_send,
    rows_recv,
    z_send,
    z_recv,
    a_send,
    a_recv,
    hp_send,
    hp_recv,
    s_send,
    s_recv,
):
    lane = lax.axis_index("dp")
    layer = lax.axis_index("pipe")
    width, rank = d_v.shape
    tokens = u_acc.shape[1]
    group = z_in.shape[1]
    half = group // 2
    queries = hc_ref.shape[1]
    every = group * n_dp
    wide = width // CHUNKS
    piece = width // PIECES
    n_example = len_ref.shape[0]

    def load_expand(c):
        cols = pl.ds(c * wide, wide)
        return pltpu.make_async_copy(e_hbm.at[0, :, cols], e_v.at[:, cols], load_e.at[c])

    def load_down(c):
        rows = pl.ds(c * wide, wide)
        return pltpu.make_async_copy(d_hbm.at[0, rows, :], d_v.at[rows, :], load_d.at[c])

    def load_cotangent(k):
        cols = pl.ds(pl.multiple_of(k * piece, piece), piece)
        return pltpu.make_async_copy(cot_hbm.at[:, cols], cot_v.at[k], load_cot.at[k])

    def load_activation(k):
        cols = pl.ds(pl.multiple_of(k * piece, piece), piece)
        return pltpu.make_async_copy(x_hbm.at[0, :, cols], x_v.at[k], load_x.at[k])

    for c in range(CHUNKS):
        load_expand(c).start()
    for c in range(CHUNKS):
        load_down(c).start()
    for k in range(PIECES):
        load_cotangent(k).start()
    for k in range(PIECES):
        load_activation(k).start()

    barrier = pltpu.get_barrier_semaphore()
    for k in range(1, n_dp):
        pl.semaphore_signal(
            barrier, 1, device_id={"dp": lax.rem(lane + k, n_dp)}, device_id_type=MESH
        )
    for k in range(1, n_pipe):
        pl.semaphore_signal(
            barrier, 1, device_id={"pipe": lax.rem(layer + k, n_pipe)}, device_id_type=MESH
        )
    pl.semaphore_wait(barrier, n_dp + n_pipe - 2)

    v_rows = v_ref[0].astype(F32)
    rows_all[lane] = jnp.concatenate([v_rows, i_ref[0].astype(F32)], axis=0).astype(BF16)

    def rows_copy(k):
        return pltpu.make_async_remote_copy(
            src_ref=rows_all.at[lane],
            dst_ref=rows_all.at[lane],
            send_sem=rows_send.at[k],
            recv_sem=rows_recv,
            device_id={"dp": lax.rem(lane + k, n_dp)},
            device_id_type=MESH,
        )

    for k in range(1, n_dp):
        rows_copy(k).start()

    def placed(first):
        row = lax.broadcasted_iota(jnp.int32, (every, queries), 0)
        col = lax.broadcasted_iota(jnp.int32, (every, queries), 1)
        within = lax.rem(row, group) - first
        query = (row // group) * half + within
        hit = (within >= 0) & (within < half) & (query == col)
        return jnp.where(hit, 1.0, 0.0).astype(BF16)

    hc_placed = jnp.dot(placed(0), hc_ref[0], preferred_element_type=F32).astype(BF16)
    ic_placed = jnp.dot(placed(half), ic_ref[0], preferred_element_type=F32).astype(BF16)
    row = lax.broadcasted_iota(jnp.int32, (group, queries), 0)
    col = lax.broadcasted_iota(jnp.int32, (group, queries), 1)
    pick = jnp.where((row >= half) & (lane * half + row - half == col), 1.0, 0.0).astype(BF16)
    ic_lane = jnp.dot(pick, ic_ref[0], preferred_element_type=F32).astype(BF16)
    v_wide = jnp.concatenate([v_rows, jnp.zeros_like(v_rows)], axis=0)

    def z_copy(step, c):
        cols = pl.ds(c * wide, wide)
        return pltpu.make_async_remote_copy(
            src_ref=z_out.at[lax.rem(step, 2), :, cols],
            dst_ref=z_in.at[step, :, cols],
            send_sem=z_send.at[c],
            recv_sem=z_recv.at[step, c],
            device_id={"pipe": lax.rem(layer + 1, n_pipe)},
            device_id_type=MESH,
        )

    has_next = layer < n_pipe - 1

    for c in range(CHUNKS):
        cols = slice(c * wide, (c + 1) * wide)
        load_expand(c).wait()
        born = v_wide[:, cols] + jnp.dot(ic_lane, e_v[:, cols], preferred_element_type=F32)
        z_out[0, :, cols] = born.astype(BF16)

        @pl.when(has_next)
        def _():
            z_copy(0, c).start()

    for c in range(CHUNKS):
        load_down(c).wait()

    def a_copy(step, k):
        return pltpu.make_async_remote_copy(
            src_ref=a_all.at[step, lane],
            dst_ref=a_all.at[step, lane],
            send_sem=a_send.at[k],
            recv_sem=a_recv.at[step],
            device_id={"dp": lax.rem(lane + k, n_dp)},
            device_id_type=MESH,
        )

    def chain(step):
        projected = jnp.zeros((group, rank), F32)
        for c in range(CHUNKS):
            cols = slice(c * wide, (c + 1) * wide)
            z_copy(step - 1, c).wait_recv()
            projected += jnp.dot(
                z_in[step - 1, :, cols], d_v[cols, :], preferred_element_type=F32
            )
        factor = (ADAPTER_SCALE * projected).astype(BF16)

        @pl.when(has_next)
        def _():
            slot = lax.rem(step, 2)
            for c in range(CHUNKS):
                cols = slice(c * wide, (c + 1) * wide)
                moved = z_in[step - 1, :, cols].astype(F32) + jnp.dot(
                    factor, e_v[:, cols], preferred_element_type=F32
                )
                z_out[slot, :, cols] = moved.astype(BF16)
                z_copy(step - 1, c).wait_send()
                z_copy(step, c).start()

        a_all[step, lane] = factor
        for k in range(1, n_dp):

            @pl.when(step > 1)
            def _():
                a_copy(step - 1, k).wait_send()

            a_copy(step, k).start()

    def token_part(k):
        load_cotangent(k).wait()
        cols = pl.ds(pl.multiple_of(k * piece, piece), piece)
        u_acc[...] += nt(e_v[:, cols], cot_v[k])

    def row_part(k):
        load_activation(k).wait()
        cols = pl.ds(pl.multiple_of(k * piece, piece), piece)
        gathered = rows_all[:, :, cols].astype(F32).reshape(every, piece)
        of_value = lax.rem(lax.broadcasted_iota(jnp.int32, (every, piece), 0), group) < half
        value_side = jnp.where(of_value, gathered, 0.0).astype(BF16)
        own_acc[...] += nt(value_side, cot_v[k])
        hidden_side = nt(hc_placed, d_v[cols, :])
        input_side = (hidden_side + jnp.where(of_value, 0.0, gathered)).astype(BF16)
        hp_acc[...] += nt(input_side, x_v[k])

    def hp_copy(target):
        return pltpu.make_async_remote_copy(
            src_ref=hp_all.at[layer],
            dst_ref=hp_all.at[layer],
            send_sem=hp_send.at[target],
            recv_sem=hp_recv.at[layer],
            device_id={"pipe": target},
            device_id_type=MESH,
        )

    def settle():
        token = lax.broadcasted_iota(jnp.int32, (every, tokens), 1)
        count = jnp.zeros((every, tokens), jnp.int32)
        for e in range(n_example):
            count = jnp.where(token // SLOT == e, len_ref[e], count)
        live = jnp.where(lax.rem(token, SLOT) < count, 1.0, 0.0)
        hp_all[layer] = (hp_acc[...] * live).astype(BF16)
        for target in range(1, n_pipe):

            @pl.when(layer < target)
            def _():
                hp_copy(target).start()

        u_bf[...] = u_acc[...].astype(BF16)
        own = own_acc[...] + jnp.dot(ic_placed, u_bf[...], preferred_element_type=F32)
        total[...] = own * hp_all[layer].astype(F32)

    def collect(step):
        @pl.when(layer >= step)
        def _():
            source = jnp.maximum(layer - step, 0)
            pltpu.make_async_copy(
                a_all.at[step, pl.ds(0, n_dp - 1)], a_all.at[step, pl.ds(0, n_dp - 1)], a_recv.at[step]
            ).wait()
            pltpu.make_async_copy(hp_all.at[source], hp_all.at[source], hp_recv.at[source]).wait()
            factors = a_all[step].astype(F32).reshape(every, rank).astype(BF16)
            total[...] += jnp.dot(factors, u_bf[...], preferred_element_type=F32) * hp_all[
                source
            ].astype(F32)

    u_acc[...] = jnp.zeros_like(u_acc)
    own_acc[...] = jnp.zeros_like(own_acc)
    hp_acc[...] = jnp.zeros_like(hp_acc)

    last_row = HEAD + PIECES
    per_step = 3

    def advance(step, carry):
        @pl.when(layer >= step)
        def _():
            chain(step)

        @pl.when(step <= PIECES)
        def _():
            token_part(jnp.minimum(step - 1, PIECES - 1))

        @pl.when(step == HEAD + 1)
        def _():
            rows_full = rows_all.at[pl.ds(0, n_dp - 1)]
            pltpu.make_async_copy(rows_full, rows_full, rows_recv).wait()

        @pl.when((step > HEAD) & (step <= last_row))
        def _():
            row_part(jnp.clip(step - 1 - HEAD, 0, PIECES - 1))

        @pl.when(step == last_row)
        def _():
            settle()

        return carry

    lax.fori_loop(1, last_row + 1, advance, 0)

    def advance_late(step, carry):
        @pl.when(layer >= step)
        def _():
            chain(step)

        first = (step - last_row - 1) * per_step
        for i in range(1, per_step + 1):

            @pl.when(first + i < n_pipe - per_step)
            def _():
                collect(jnp.minimum(first + i, n_pipe - 1))

        return carry

    lax.fori_loop(last_row + 1, n_pipe, advance_late, 0)
    for step in range(n_pipe - per_step, n_pipe):
        collect(step)

    row = lax.broadcasted_iota(jnp.int32, (8, tokens), 0)
    token = lax.broadcasted_iota(jnp.int32, (8, tokens), 1)
    members = jnp.where(token // SLOT == row, 1.0, 0.0)
    sums = lax.dot_general(
        members,
        total[...],
        (((1,), (1,)), ((), ())),
        precision=lax.Precision.HIGHEST,
        preferred_element_type=F32,
    )
    row = lax.broadcasted_iota(jnp.int32, (every, 128), 0)
    col = lax.broadcasted_iota(jnp.int32, (every, 128), 1)
    joined = jnp.where((row // group) * half + lax.rem(row, half) == col, 1.0, 0.0)
    s_all[layer] = jnp.dot(
        sums, joined, precision=lax.Precision.HIGHEST, preferred_element_type=F32
    )

    def s_copy(k):
        return pltpu.make_async_remote_copy(
            src_ref=s_all.at[layer],
            dst_ref=s_all.at[layer],
            send_sem=s_send.at[k],
            recv_sem=s_recv,
            device_id={"pipe": lax.rem(layer + k, n_pipe)},
            device_id_type=MESH,
        )

    for k in range(1, n_pipe):
        s_copy(k).start()

    for k in range(1, n_dp):
        rows_copy(k).wait_send()

        @pl.when(layer >= 1)
        def _():
            a_copy(layer, k).wait_send()

    @pl.when(has_next)
    def _():
        for c in range(CHUNKS):
            z_copy(layer, c).wait_send()

    for target in range(1, n_pipe):

        @pl.when(layer < target)
        def _():
            hp_copy(target).wait_send()

    for k in range(1, n_pipe):
        s_copy(k).wait_send()
    arrived = s_all.at[pl.ds(0, n_pipe - 1)]
    pltpu.make_async_copy(arrived, arrived, s_recv).wait()
    result = s_all[0]
    for source in range(1, n_pipe):
        result = result + s_all[source]
    result = result[:n_example, :queries] * (ADAPTER_SCALE * SLOT**-0.5)
    example = lane * n_example + lax.broadcasted_iota(jnp.int32, (n_example, queries), 0)
    out_ref[...] = result * jnp.where(example != qe_ref[...], 1.0, 0.0)


def solution(mesh):
    n_dp, n_pipe = mesh.shape["dp"], mesh.shape["pipe"]

    def local(act, cot, down, expand, value, inputs, hidden_cols, inner_cols, lengths, query):
        tokens, width = cot.shape
        rank = down.shape[2]
        queries = hidden_cols.shape[1]
        n_example = tokens // SLOT
        group = 2 * value.shape[1]
        every = group * n_dp
        hbm = pl.BlockSpec(memory_space=pl.ANY)
        vmem = pl.BlockSpec(memory_space=pltpu.VMEM)
        smem = pl.BlockSpec(memory_space=pltpu.SMEM)
        dma = pltpu.SemaphoreType.DMA
        return pl.pallas_call(
            functools.partial(kernel, n_dp, n_pipe),
            out_shape=jax.ShapeDtypeStruct((n_example, queries), F32),
            in_specs=[hbm, hbm, hbm, hbm, vmem, vmem, vmem, vmem, smem, vmem],
            out_specs=vmem,
            scratch_shapes=[
                pltpu.VMEM((PIECES, tokens, width // PIECES), BF16),
                pltpu.VMEM((PIECES, tokens, width // PIECES), BF16),
                pltpu.VMEM((width, rank), BF16),
                pltpu.VMEM((rank, width), BF16),
                pltpu.VMEM((n_pipe, group, width), BF16),
                pltpu.VMEM((2, group, width), BF16),
                pltpu.VMEM((n_pipe, n_dp, group, rank), BF16),
                pltpu.VMEM((n_pipe, every, tokens), BF16),
                pltpu.VMEM((n_dp, group, width), BF16),
                pltpu.VMEM((rank, tokens), F32),
                pltpu.VMEM((rank, tokens), BF16),
                pltpu.VMEM((every, tokens), F32),
                pltpu.VMEM((every, tokens), F32),
                pltpu.VMEM((every, tokens), F32),
                pltpu.VMEM((n_pipe, 8, 128), F32),
                dma((CHUNKS,)),
                dma((CHUNKS,)),
                dma((PIECES,)),
                dma((PIECES,)),
                dma((n_dp,)),
                dma,
                dma((CHUNKS,)),
                dma((n_pipe, CHUNKS)),
                dma((n_dp,)),
                dma((n_pipe,)),
                dma((n_pipe,)),
                dma((n_pipe,)),
                dma((n_pipe,)),
                dma,
            ],
            compiler_params=pltpu.CompilerParams(
                collective_id=0, has_side_effects=True, vmem_limit_bytes=58 << 20
            ),
            name="influence",
        )(
            act,
            cot,
            down,
            expand,
            value,
            inputs,
            hidden_cols,
            inner_cols,
            lengths,
            query.reshape(1, queries),
        )

    in_specs = (
        P("pipe", "dp", None),
        P("dp", None),
        P("pipe", None, None),
        P("pipe", None, None),
        P("pipe", "dp", None),
        P("pipe", "dp", None),
        P("pipe", None, None),
        P("pipe", None, None),
        P("dp"),
        P(),
    )
    return jax.shard_map(
        local, mesh=mesh, in_specs=in_specs, out_specs=P("dp", None), check_vma=False
    )
```

time: 914 us -> 95.4 us (0.10)
  waiting for transfers between devices: 631 us -> 0 us
  blocking collectives: 111 us -> 0 us
  Pallas kernels: 0 us -> 94 us
  matrix products: 77.8 us -> 0 us
  starting transfers between devices: 46.8 us -> 0 us
  local copies, waits for them, and re-layouts: 27.1 us -> 1.26 us
  other arithmetic: 13.2 us -> 0 us
    ppermute x19 -> x0, waiting for transfers between devices: 631 us -> none  [from_behind(): lax.ppermute(value, axis, [(source, source + steps) for source in range(f...]
    pallas_call x0 -> x1, Pallas kernels: none -> 94 us  [local(): pl.pallas_call(functools.partial(kernel, n_dp, n_pipe), out_shape=jax.Sha...]
    dot_general x24 -> x0, matrix products: 77.8 us -> none  [the longest x4 25.8 us: compute(): jnp.einsum('td,rd->tr', gradient_leaving, up_map, preferred_element_type=...]
    psum x1 -> x0, blocking collectives: 59.4 us -> none  [local(): totals = lax.psum(local_sums, 'pipe') * SLOT ** (-0.5)]
    all_gather x2 -> x0, blocking collectives: 52.1 us -> none  [the longest x1 26.8 us: local(): lax.all_gather(value_rows[0], 'dp', axis=0, tiled=True)]
    ppermute x19 -> x0, starting transfers between devices: 46.8 us -> none  [from_behind(): lax.ppermute(value, axis, [(source, source + steps) for source in range(f...]
    another operation x31 -> x0, local copies, waits for them, and re-layouts: 23.5 us -> none
    select_n x4 -> x0, other arithmetic: 10.1 us -> none  [advance(): gradient_leaving = jnp.where(is_last, seed_rows, incoming)]
  transfers between devices with their start and end apart: 19 -> 0, of which waited for: 19 -> 0; matrix products, arithmetic and copies ran while one was open for 0% -> 0% of each run, Pallas kernels for 0% -> 0%
where the time goes in v1:
time: 95.4 us; the launch traced here: 95.3 us
  Pallas kernels  94 us (99%)
  local copies, waits for them, and re-layouts  1.26 us (1%)
    pallas_call x1, Pallas kernels, local(): pl.pallas_call(functools.partial(kernel, n_dp, n_pipe), out_shape=jax.Sha...  94 us

profile of v1, /device:TPU:1, one launch (start us, length us, event | category | flops | bytes accessed | tf_op | source)
XLA Modules:
  0.0 95.3 jit_solution(15959063702075581648)
XLA Ops:
  0.0 94.0 %influence.1 = f32[4,32]{1,0:T(4,128)} custom-call(bf16[1,512,8192]{2,1,0:T(8,128)(2,1)} %x_hbm.1, bf16[512,8192]{1,0:T(8,128)(2,1)} %cot_hbm.1, bf16[1,8192,512]{2,1,0:T(8,128)(2,1)} %d_hbm.1, bf16[1,512,8192]{2,1,0:T(8,128)(2,1)} %e_hbm.1, bf16[1,4,8192]{2,1,0:T(4,128)(2,1)} %v_ref.1, bf16[1,4,8192]{2,1,0:T(4,128)(2,1)} %i_ref.1, ...), custom_call_target="tpu_custom_call" | custom-call | tf_op jit(solution)/shard_map/influence/pallas_call | solution.py:396
  94.0 1.3 %copy.12 = f32[4,32]{1,0:T(4,128)} copy(f32[4,32]{1,0:T(4,128)} %influence.1) | data formatting | bytes 1024

commit v2 on v1

--- a/solution.py
+++ b/solution.py
@@ -14,6 +14,7 @@
 BF16 = jnp.bfloat16
 CHUNKS = 4
 PIECES = 8
+LOW = 6
 HEAD = 2
 
 
@@ -272,52 +273,55 @@
     own_acc[...] = jnp.zeros_like(own_acc)
     hp_acc[...] = jnp.zeros_like(hp_acc)
 
-    last_row = HEAD + PIECES
+    begin = jnp.where(layer < LOW, layer, 0)
+    row_begin = jnp.maximum(begin, HEAD)
     per_step = 3
+    first_collect = n_pipe - n_pipe // per_step
 
     def advance(step, carry):
         @pl.when(layer >= step)
         def _():
             chain(step)
 
-        @pl.when(step <= PIECES)
-        def _():
-            token_part(jnp.minimum(step - 1, PIECES - 1))
-
-        @pl.when(step == HEAD + 1)
+        @pl.when((step > begin) & (step <= begin + PIECES))
+        def _():
+            token_part(jnp.clip(step - 1 - begin, 0, PIECES - 1))
+
+        @pl.when(step == row_begin + 1)
         def _():
             rows_full = rows_all.at[pl.ds(0, n_dp - 1)]
             pltpu.make_async_copy(rows_full, rows_full, rows_recv).wait()
 
-        @pl.when((step > HEAD) & (step <= last_row))
-        def _():
-            row_part(jnp.clip(step - 1 - HEAD, 0, PIECES - 1))
-
-        @pl.when(step == last_row)
+        @pl.when((step > row_begin) & (step <= row_begin + PIECES))
+        def _():
+            row_part(jnp.clip(step - 1 - row_begin, 0, PIECES - 1))
+
+        @pl.when(step == row_begin + PIECES)
         def _():
             settle()
 
+        @pl.when((step >= first_collect) & (layer >= LOW))
+        def _():
+            first = (step - first_collect) * per_step
+            for i in range(1, per_step + 1):
+
+                @pl.when(first + i < n_pipe - per_step)
+                def _():
+                    collect(jnp.clip(first + i, 1, n_pipe - 1))
+
         return carry
 
-    lax.fori_loop(1, last_row + 1, advance, 0)
-
-    def advance_late(step, carry):
-        @pl.when(layer >= step)
-        def _():
-            chain(step)
-
-        first = (step - last_row - 1) * per_step
-        for i in range(1, per_step + 1):
-
-            @pl.when(first + i < n_pipe - per_step)
-            def _():
-                collect(jnp.minimum(first + i, n_pipe - 1))
-
-        return carry
-
-    lax.fori_loop(last_row + 1, n_pipe, advance_late, 0)
-    for step in range(n_pipe - per_step, n_pipe):
-        collect(step)
+    lax.fori_loop(1, n_pipe, advance, 0)
+
+    @pl.when(layer < LOW)
+    def _():
+        for step in range(1, LOW):
+            collect(step)
+
+    @pl.when(layer >= LOW)
+    def _():
+        for step in range(n_pipe - per_step, n_pipe):
+            collect(step)
 
     row = lax.broadcasted_iota(jnp.int32, (8, tokens), 0)
     token = lax.broadcasted_iota(jnp.int32, (8, tokens), 1)

time: 95.4 us -> 95.6 us (level)
  no operation moved by 1% of the time
where the time goes in v2:
time: 95.6 us; the launch traced here: 95.4 us
  Pallas kernels  94.2 us (99%)
  local copies, waits for them, and re-layouts  1.26 us (1%)
    pallas_call x1, Pallas kernels, local(): pl.pallas_call(functools.partial(kernel, n_dp, n_pipe), out_shape=jax.Sha...  94.2 us

profile of v2, /device:TPU:1, one launch (start us, length us, event | category | flops | bytes accessed | tf_op | source)
XLA Modules:
  0.0 95.4 jit_solution(326548029432903005)
XLA Ops:
  0.0 94.2 %influence.1 = f32[4,32]{1,0:T(4,128)} custom-call(bf16[1,512,8192]{2,1,0:T(8,128)(2,1)} %x_hbm.1, bf16[512,8192]{1,0:T(8,128)(2,1)} %cot_hbm.1, bf16[1,8192,512]{2,1,0:T(8,128)(2,1)} %d_hbm.1, bf16[1,512,8192]{2,1,0:T(8,128)(2,1)} %e_hbm.1, bf16[1,4,8192]{2,1,0:T(4,128)(2,1)} %v_ref.1, bf16[1,4,8192]{2,1,0:T(4,128)(2,1)} %i_ref.1, ...), custom_call_target="tpu_custom_call" | custom-call | tf_op jit(solution)/shard_map/influence/pallas_call | solution.py:400
  94.2 1.3 %copy.12 = f32[4,32]{1,0:T(4,128)} copy(f32[4,32]{1,0:T(4,128)} %influence.1) | data formatting | bytes 1024

commit v3 on v1

v3 whole, which is shorter than its diff:
```python
import functools

import jax
import jax.numpy as jnp
from jax import lax
from jax.experimental import pallas as pl
from jax.experimental.pallas import tpu as pltpu
from jax.sharding import PartitionSpec as P

SLOT = 128
ADAPTER_SCALE = 0.25
MESH = pl.DeviceIdType.MESH
F32 = jnp.float32
BF16 = jnp.bfloat16
CHUNKS = 4
PIECES = 8
ALONE = 1
LOW = 3


def nt(a, b):
    return lax.dot_general(a, b, (((1,), (1,)), ((), ())), preferred_element_type=F32)


def kernel(
    n_dp,
    n_pipe,
    x_hbm,
    cot_hbm,
    d_hbm,
    e_hbm,
    v_ref,
    i_ref,
    hc_ref,
    ic_ref,
    len_ref,
    qe_ref,
    out_ref,
    x_v,
    cot_v,
    d_v,
    e_v,
    z_in,
    y_in,
    sent,
    a_all,
    f_in,
    k_part,
    k_all,
    hp_all,
    rows_all,
    u_acc,
    u_bf,
    own_acc,
    hp_acc,
    total,
    s_all,
    load_e,
    load_d,
    load_cot,
    load_x,
    rows_send,
    rows_recv,
    main_send,
    pass_send,
    z_recv,
    y_recv,
    f_send,
    f_recv,
    part_send,
    part_recv,
    k_send,
    k_recv,
    a_send,
    a_recv,
    hp_send,
    pass_hp,
    hp_recv,
    s_send,
    s_recv,
):
    lane = lax.axis_index("dp")
    layer = lax.axis_index("pipe")
    core = lax.rem(layer, 2)
    chip = layer // 2
    n_chip = n_pipe // 2
    is_top = chip == n_chip - 1
    width, rank = d_v.shape
    tokens = u_acc.shape[1]
    group = z_in.shape[1]
    half = group // 2
    queries = hc_ref.shape[1]
    every = group * n_dp
    share = rank // n_dp
    wide = width // CHUNKS
    piece = width // PIECES
    n_example = len_ref.shape[0]
    sibling = {"pipe": layer + 1 - 2 * core}
    above = {"pipe": lax.rem(2 * chip + 2, n_pipe)}

    def span(c):
        return slice(c * wide, (c + 1) * wide)

    def remote(src, dst, send_sem, recv_sem, device):
        return pltpu.make_async_remote_copy(
            src_ref=src,
            dst_ref=dst,
            send_sem=send_sem,
            recv_sem=recv_sem,
            device_id=device,
            device_id_type=MESH,
        )

    def landed(ref, sem):
        pltpu.make_async_copy(ref, ref, sem).wait()

    def load_expand(c):
        cols = pl.ds(c * wide, wide)
        return pltpu.make_async_copy(e_hbm.at[0, :, cols], e_v.at[:, cols], load_e.at[c])

    def load_down(c):
        rows = pl.ds(c * wide, wide)
        return pltpu.make_async_copy(d_hbm.at[0, rows, :], d_v.at[rows, :], load_d.at[c])

    def load_cotangent(k):
        cols = pl.ds(pl.multiple_of(k * piece, piece), piece)
        return pltpu.make_async_copy(cot_hbm.at[:, cols], cot_v.at[k], load_cot.at[k])

    def load_activation(k):
        cols = pl.ds(pl.multiple_of(k * piece, piece), piece)
        return pltpu.make_async_copy(x_hbm.at[0, :, cols], x_v.at[k], load_x.at[k])

    for c in range(CHUNKS):
        load_expand(c).start()
    for c in range(CHUNKS):
        load_down(c).start()
    for k in range(PIECES):
        load_cotangent(k).start()
    for k in range(PIECES):
        load_activation(k).start()

    barrier = pltpu.get_barrier_semaphore()
    for k in range(1, n_dp):
        pl.semaphore_signal(
            barrier, 1, device_id={"dp": lax.rem(lane + k, n_dp)}, device_id_type=MESH
        )
    for k in range(1, n_pipe):
        pl.semaphore_signal(
            barrier, 1, device_id={"pipe": lax.rem(layer + k, n_pipe)}, device_id_type=MESH
        )
    pl.semaphore_wait(barrier, n_dp + n_pipe - 2)

    v_rows = v_ref[0].astype(F32)
    rows_all[lane] = jnp.concatenate([v_rows, i_ref[0].astype(F32)], axis=0).astype(BF16)

    def lane_at(k):
        return {"dp": lax.rem(lane + k, n_dp)}

    def spread_rows():
        for k in range(1, n_dp):
            remote(
                rows_all.at[lane], rows_all.at[lane], rows_send, rows_recv, lane_at(k)
            ).start()

    @pl.when(core == 0)
    def _():
        spread_rows()

    row = lax.broadcasted_iota(jnp.int32, (group, queries), 0)
    col = lax.broadcasted_iota(jnp.int32, (group, queries), 1)
    pick = jnp.where((row >= half) & (lane * half + row - half == col), 1.0, 0.0).astype(BF16)
    ic_lane = jnp.dot(pick, ic_ref[0], preferred_element_type=F32).astype(BF16)
    v_wide = jnp.concatenate([v_rows, jnp.zeros_like(v_rows)], axis=0)

    def own_copy(c):
        return remote(
            sent.at[layer, :, span(c)],
            z_in.at[layer, :, span(c)],
            main_send.at[layer, c],
            z_recv.at[layer, c],
            sibling,
        )

    def up_copy(u, n, c):
        rows = pl.ds(u, n)
        return remote(
            sent.at[rows, :, span(c)],
            z_in.at[rows, :, span(c)],
            main_send.at[u, c],
            z_recv.at[u, c],
            above,
        )

    def over_copy(u, n, c):
        rows = pl.ds(u, n)
        return remote(
            sent.at[rows, :, span(c)],
            y_in.at[rows, :, span(c)],
            main_send.at[u, c],
            y_recv.at[u, c],
            sibling,
        )

    def pass_copy(u, n, c):
        rows = pl.ds(u, n)
        return remote(
            z_in.at[rows, :, span(c)],
            z_in.at[rows, :, span(c)],
            pass_send.at[u, c],
            z_recv.at[u, c],
            sibling,
        )

    def factor_copy(u, n):
        rows = pl.ds(u, n)
        return remote(a_all.at[lane, rows], f_in.at[rows], f_send.at[u], f_recv.at[u], sibling)

    def spread_factors(u, n):
        rows = pl.ds(u, n)
        for k in range(1, n_dp):
            remote(
                a_all.at[lane, rows], a_all.at[lane, rows], a_send.at[u], a_recv.at[u], lane_at(k)
            ).start()

    others = pl.ds(0, n_dp - 1)

    def part_copy(c):
        return remote(
            e_v.at[pl.ds(pl.multiple_of(lane * share, share), share), span(c)],
            k_part.at[:, span(c)],
            part_send.at[c],
            part_recv.at[c],
            sibling,
        )

    is_lower = core == 0
    is_upper = core == 1
    pairs_up = chip >= ALONE

    for c in range(CHUNKS):
        load_expand(c).wait()
        born = v_wide[:, span(c)] + jnp.dot(ic_lane, e_v[:, span(c)], preferred_element_type=F32)
        sent[layer, :, span(c)] = born.astype(BF16)

        @pl.when(is_lower)
        def _():
            own_copy(c).start()

        @pl.when(is_lower & (chip > 0))
        def _():
            part_copy(c).start()

        @pl.when(is_upper & jnp.logical_not(pairs_up))
        def _():
            up_copy(layer, 1, c).start()

    for c in range(CHUNKS):
        load_down(c).wait()

    def take(ref, u, n, c):
        return ref[pl.ds(u, n), :, span(c)].astype(F32).reshape(n * group, wide)

    def down(z, c):
        return jnp.dot(z.astype(BF16), d_v[span(c), :], preferred_element_type=F32)

    def up(factor, c):
        return jnp.dot(factor, e_v[:, span(c)], preferred_element_type=F32)

    def keep(u, n, projected):
        factor = ADAPTER_SCALE * projected
        a_all[lane, pl.ds(u, n)] = factor.reshape(n, group, rank).astype(BF16)
        return factor.astype(BF16)

    def put(u, n, c, moved):
        sent[pl.ds(u, n), :, span(c)] = moved.reshape(n, group, wide).astype(BF16)

    def lower_stage(u, n):
        projected = jnp.zeros((n * group, rank), F32)
        for c in range(CHUNKS):
            up_copy(u, n, c).wait_recv()
            pass_copy(u, n, c).start()
            projected += down(take(z_in, u, n, c), c)
        factor = keep(u, n, projected)
        factor_copy(u, n).start()

        @pl.when(jnp.logical_not(is_top))
        def _():
            for c in range(CHUNKS):
                put(u, n, c, take(z_in, u, n, c) + up(factor, c))
                over_copy(u, n, c).start()

        spread_factors(u, n)

    def upper_stage(u, n):
        projected = jnp.zeros((n * group, rank), F32)
        for c in range(CHUNKS):
            pass_copy(u, n, c).wait_recv()
            projected += down(take(z_in, u, n, c), c)
        factor_copy(u, n).wait_recv()
        below = f_in[pl.ds(u, n)].astype(F32).reshape(n * group, rank).astype(BF16)
        projected += jnp.dot(below, k_all[...].reshape(rank, rank), preferred_element_type=F32)
        factor = keep(u, n, projected)

        @pl.when(jnp.logical_not(is_top))
        def _():
            for c in range(CHUNKS):
                over_copy(u, n, c).wait_recv()
                put(u, n, c, take(y_in, u, n, c) + up(factor, c))
                up_copy(u, n, c).start()

        spread_factors(u, n)

    @pl.when(is_upper)
    def _():
        u = layer - 1
        projected = jnp.zeros((group, rank), F32)
        for c in range(CHUNKS):
            landed(z_in.at[u, :, span(c)], z_recv.at[u, c])
            projected += down(take(z_in, u, 1, c), c)
        factor = keep(u, 1, projected)

        @pl.when(jnp.logical_not(is_top))
        def _():
            for c in range(CHUNKS):
                put(u, 1, c, take(z_in, u, 1, c) + up(factor, c))

                @pl.when(pairs_up)
                def _():
                    up_copy(u, 2, c).start()

                @pl.when(jnp.logical_not(pairs_up))
                def _():
                    up_copy(u, 1, c).start()

        @pl.when(chip > 0)
        def _():
            coupled = jnp.zeros((share, rank), F32)
            for c in range(CHUNKS):
                landed(k_part.at[:, span(c)], part_recv.at[c])
                coupled += jnp.dot(k_part[:, span(c)], d_v[span(c), :], preferred_element_type=F32)
            k_all[lane] = coupled.astype(BF16)
            for k in range(1, n_dp):
                remote(k_all.at[lane], k_all.at[lane], k_send, k_recv, lane_at(k)).start()

        spread_factors(u, 1)
        spread_rows()

    def placed(first):
        row = lax.broadcasted_iota(jnp.int32, (every, queries), 0)
        col = lax.broadcasted_iota(jnp.int32, (every, queries), 1)
        within = lax.rem(row, group) - first
        query = (row // group) * half + within
        hit = (within >= 0) & (within < half) & (query == col)
        return jnp.where(hit, 1.0, 0.0).astype(BF16)

    hc_placed = jnp.dot(placed(0), hc_ref[0], preferred_element_type=F32).astype(BF16)
    ic_placed = jnp.dot(placed(half), ic_ref[0], preferred_element_type=F32).astype(BF16)
    def token_part(k):
        load_cotangent(k).wait()
        cols = pl.ds(pl.multiple_of(k * piece, piece), piece)
        u_acc[...] += nt(e_v[:, cols], cot_v[k])

    def row_part(k):
        load_activation(k).wait()
        cols = pl.ds(pl.multiple_of(k * piece, piece), piece)
        gathered = rows_all[:, :, cols].astype(F32).reshape(every, piece)
        of_value = lax.rem(lax.broadcasted_iota(jnp.int32, (every, piece), 0), group) < half
        value_side = jnp.where(of_value, gathered, 0.0).astype(BF16)
        own_acc[...] += nt(value_side, cot_v[k])
        hidden_side = nt(hc_placed, d_v[cols, :])
        input_side = (hidden_side + jnp.where(of_value, 0.0, gathered)).astype(BF16)
        hp_acc[...] += nt(input_side, x_v[k])

    def hp_copy(target):
        return remote(
            hp_all.at[layer],
            hp_all.at[layer],
            hp_send.at[target],
            hp_recv.at[layer],
            {"pipe": 2 * target + core},
        )

    def hp_pass(source):
        return remote(
            hp_all.at[source], hp_all.at[source], pass_hp.at[source], hp_recv.at[source], sibling
        )

    def settle():
        token = lax.broadcasted_iota(jnp.int32, (every, tokens), 1)
        count = jnp.zeros((every, tokens), jnp.int32)
        for e in range(n_example):
            count = jnp.where(token // SLOT == e, len_ref[e], count)
        live = jnp.where(lax.rem(token, SLOT) < count, 1.0, 0.0)
        hp_all[layer] = (hp_acc[...] * live).astype(BF16)
        for target in range(1, n_chip):

            @pl.when(chip < target)
            def _():
                hp_copy(target).start()

        @pl.when(is_lower)
        def _():
            hp_pass(layer).start()

        u_bf[...] = u_acc[...].astype(BF16)
        own = own_acc[...] + jnp.dot(ic_placed, u_bf[...], preferred_element_type=F32)
        total[...] = own * hp_all[layer].astype(F32)

    def add(source):
        factors = a_all[:, source].astype(F32).reshape(every, rank).astype(BF16)
        total[...] += jnp.dot(factors, u_bf[...], preferred_element_type=F32) * hp_all[
            source
        ].astype(F32)

    def collect(below):
        mine, other = 2 * below + core, 2 * below + 1 - core
        landed(hp_all.at[mine], hp_recv.at[mine])
        hp_pass(mine).start()
        landed(hp_all.at[other], hp_recv.at[other])

        @pl.when(below >= ALONE)
        def _():
            landed(a_all.at[others, pl.ds(2 * below, 2)], a_recv.at[2 * below])

        @pl.when(below < ALONE)
        def _():
            landed(a_all.at[others, pl.ds(2 * below + 1, 1)], a_recv.at[2 * below + 1])

        add(2 * below + 1)

        @pl.when(below < ALONE)
        def _():
            landed(a_all.at[others, pl.ds(2 * below, 1)], a_recv.at[2 * below])

        add(2 * below)

    u_acc[...] = jnp.zeros_like(u_acc)
    own_acc[...] = jnp.zeros_like(own_acc)
    hp_acc[...] = jnp.zeros_like(hp_acc)
    hc_placed = jnp.dot(placed(0), hc_ref[0], preferred_element_type=F32).astype(BF16)
    ic_placed = jnp.dot(placed(half), ic_ref[0], preferred_element_type=F32).astype(BF16)

    is_low = chip < LOW

    def token_end(step):
        late = jnp.where(step >= chip, PIECES, 0)
        return jnp.where(is_low, late, jnp.clip(4 + 2 * step, 0, PIECES))

    def row_end(step):
        late = jnp.where(step >= chip, PIECES, 0)
        return jnp.where(is_low, late, jnp.clip(2 * step - 2, 0, PIECES))

    def token_side(step, before_token, before_row):
        end_token, end_row = token_end(step), row_end(step)

        def token_step(k, carry):
            token_part(k)
            return carry

        def row_step(k, carry):
            row_part(k)
            return carry

        lax.fori_loop(before_token, end_token, token_step, 0)

        @pl.when((before_row == 0) & (end_row > 0))
        def _():
            landed(rows_all.at[others], rows_recv)

        lax.fori_loop(before_row, end_row, row_step, 0)

        @pl.when((before_row < PIECES) & (end_row == PIECES))
        def _():
            settle()

    def stage(u, n):
        @pl.when(is_lower)
        def _():
            lower_stage(u, n)

        @pl.when(is_upper)
        def _():
            upper_stage(u, n)

    def collect_down(first, last):
        def body(i, carry):
            collect(first - i)
            return carry

        lax.fori_loop(0, jnp.maximum(first - last + 1, 0), body, 0)

    early = 2

    def advance(step, carry):
        @pl.when((step >= 1) & (step <= chip))
        def _():
            below = jnp.maximum(chip - step, 0)

            @pl.when((step == 1) & is_upper)
            def _():
                landed(k_all.at[others], k_recv)

            @pl.when(below >= ALONE)
            def _():
                stage(2 * below, 2)

            @pl.when(below < ALONE)
            def _():
                def one(i, carry):
                    stage(2 * below + 1 - i, 1)
                    return carry

                lax.fori_loop(0, 2, one, 0)

        before_token = jnp.where(step == 0, 0, token_end(step - 1))
        before_row = jnp.where(step == 0, 0, row_end(step - 1))
        token_side(step, before_token, before_row)

        @pl.when((step == n_chip - 2) & is_top)
        def _():
            collect_down(n_chip - 2, early)

        return carry

    lax.fori_loop(0, n_chip, advance, 0)

    @pl.when(is_upper)
    def _():
        own = layer - 1
        landed(hp_all.at[own], hp_recv.at[own])
        landed(a_all.at[others, pl.ds(own, 1)], a_recv.at[own])
        add(own)

    collect_down(jnp.where(is_top, early - 1, chip - 1), 0)

    row = lax.broadcasted_iota(jnp.int32, (8, tokens), 0)
    token = lax.broadcasted_iota(jnp.int32, (8, tokens), 1)
    members = jnp.where(token // SLOT == row, 1.0, 0.0)
    sums = lax.dot_general(
        members,
        total[...],
        (((1,), (1,)), ((), ())),
        precision=lax.Precision.HIGHEST,
        preferred_element_type=F32,
    )
    row = lax.broadcasted_iota(jnp.int32, (every, 128), 0)
    col = lax.broadcasted_iota(jnp.int32, (every, 128), 1)
    joined = jnp.where((row // group) * half + lax.rem(row, half) == col, 1.0, 0.0)
    s_all[layer] = jnp.dot(
        sums, joined, precision=lax.Precision.HIGHEST, preferred_element_type=F32
    )

    def s_copy(k):
        return pltpu.make_async_remote_copy(
            src_ref=s_all.at[layer],
            dst_ref=s_all.at[layer],
            send_sem=s_send.at[k],
            recv_sem=s_recv,
            device_id={"pipe": lax.rem(layer + k, n_pipe)},
            device_id_type=MESH,
        )

    for k in range(1, n_pipe):
        s_copy(k).start()

    landed(rows_all.at[others], rows_send)

    def sent_unit(u, n):
        rows = pl.ds(u, n)
        landed(a_all.at[others, rows], a_send.at[u])

        @pl.when(is_lower)
        def _():
            factor_copy(u, n).wait_send()
            for c in range(CHUNKS):
                pass_copy(u, n, c).wait_send()

        @pl.when(jnp.logical_not(is_top))
        def _():
            for c in range(CHUNKS):
                up_copy(u, n, c).wait_send()

    def sent_pair(below, carry):
        sent_unit(2 * below, 2)
        return carry

    def sent_one(u, carry):
        sent_unit(u, 1)
        return carry

    lax.fori_loop(ALONE, jnp.maximum(chip, ALONE), sent_pair, 0)
    lax.fori_loop(0, jnp.minimum(2 * ALONE, 2 * chip), sent_one, 0)

    @pl.when(is_lower)
    def _():
        for c in range(CHUNKS):
            own_copy(c).wait_send()
        hp_pass(layer).wait_send()

    @pl.when(is_lower & (chip > 0))
    def _():
        for c in range(CHUNKS):
            part_copy(c).wait_send()

    @pl.when(is_upper)
    def _():
        landed(a_all.at[others, pl.ds(layer - 1, 1)], a_send.at[layer - 1])

        @pl.when(chip > 0)
        def _():
            landed(k_all.at[others], k_send)

        @pl.when(jnp.logical_not(is_top))
        def _():
            for c in range(CHUNKS):

                @pl.when(pairs_up)
                def _():
                    up_copy(layer - 1, 2, c).wait_send()

                @pl.when(jnp.logical_not(pairs_up))
                def _():
                    up_copy(layer - 1, 1, c).wait_send()
                    up_copy(layer, 1, c).wait_send()

    for target in range(1, n_chip):

        @pl.when(chip < target)
        def _():
            hp_copy(target).wait_send()

        @pl.when(chip >= target)
        def _():
            hp_pass(2 * (target - 1) + core).wait_send()

    for k in range(1, n_pipe):
        s_copy(k).wait_send()
    arrived = s_all.at[pl.ds(0, n_pipe - 1)]
    pltpu.make_async_copy(arrived, arrived, s_recv).wait()
    result = s_all[0]
    for source in range(1, n_pipe):
        result = result + s_all[source]
    result = result[:n_example, :queries] * (ADAPTER_SCALE * SLOT**-0.5)
    example = lane * n_example + lax.broadcasted_iota(jnp.int32, (n_example, queries), 0)
    out_ref[...] = result * jnp.where(example != qe_ref[...], 1.0, 0.0)


def solution(mesh):
    n_dp, n_pipe = mesh.shape["dp"], mesh.shape["pipe"]

    def local(act, cot, down, expand, value, inputs, hidden_cols, inner_cols, lengths, query):
        tokens, width = cot.shape
        rank = down.shape[2]
        queries = hidden_cols.shape[1]
        n_example = tokens // SLOT
        group = 2 * value.shape[1]
        every = group * n_dp
        hbm = pl.BlockSpec(memory_space=pl.ANY)
        vmem = pl.BlockSpec(memory_space=pltpu.VMEM)
        smem = pl.BlockSpec(memory_space=pltpu.SMEM)
        dma = pltpu.SemaphoreType.DMA
        return pl.pallas_call(
            functools.partial(kernel, n_dp, n_pipe),
            out_shape=jax.ShapeDtypeStruct((n_example, queries), F32),
            in_specs=[hbm, hbm, hbm, hbm, vmem, vmem, vmem, vmem, smem, vmem],
            out_specs=vmem,
            scratch_shapes=[
                pltpu.VMEM((PIECES, tokens, width // PIECES), BF16),
                pltpu.VMEM((PIECES, tokens, width // PIECES), BF16),
                pltpu.VMEM((width, rank), BF16),
                pltpu.VMEM((rank, width), BF16),
                pltpu.VMEM((n_pipe, group, width), BF16),
                pltpu.VMEM((n_pipe, group, width), BF16),
                pltpu.VMEM((n_pipe, group, width), BF16),
                pltpu.VMEM((n_dp, n_pipe, group, rank), BF16),
                pltpu.VMEM((n_pipe, group, rank), BF16),
                pltpu.VMEM((rank // n_dp, width), BF16),
                pltpu.VMEM((n_dp, rank // n_dp, rank), BF16),
                pltpu.VMEM((n_pipe, every, tokens), BF16),
                pltpu.VMEM((n_dp, group, width), BF16),
                pltpu.VMEM((rank, tokens), F32),
                pltpu.VMEM((rank, tokens), BF16),
                pltpu.VMEM((every, tokens), F32),
                pltpu.VMEM((every, tokens), F32),
                pltpu.VMEM((every, tokens), F32),
                pltpu.VMEM((n_pipe, 8, 128), F32),
                dma((CHUNKS,)),
                dma((CHUNKS,)),
                dma((PIECES,)),
                dma((PIECES,)),
                dma,
                dma,
                dma((n_pipe, CHUNKS)),
                dma((n_pipe, CHUNKS)),
                dma((n_pipe, CHUNKS)),
                dma((n_pipe, CHUNKS)),
                dma((n_pipe,)),
                dma((n_pipe,)),
                dma((CHUNKS,)),
                dma((CHUNKS,)),
                dma,
                dma,
                dma((n_pipe,)),
                dma((n_pipe,)),
                dma((n_pipe // 2,)),
                dma((n_pipe,)),
                dma((n_pipe,)),
                dma((n_pipe,)),
                dma,
            ],
            compiler_params=pltpu.CompilerParams(
                collective_id=0, has_side_effects=True, vmem_limit_bytes=58 << 20
            ),
            name="influence",
        )(
            act,
            cot,
            down,
            expand,
            value,
            inputs,
            hidden_cols,
            inner_cols,
            lengths,
            query.reshape(1, queries),
        )

    in_specs = (
        P("pipe", "dp", None),
        P("dp", None),
        P("pipe", None, None),
        P("pipe", None, None),
        P("pipe", "dp", None),
        P("pipe", "dp", None),
        P("pipe", None, None),
        P("pipe", None, None),
        P("dp"),
        P(),
    )
    return jax.shard_map(
        local, mesh=mesh, in_specs=in_specs, out_specs=P("dp", None), check_vma=False
    )
```

time: 95.4 us -> 88.8 us (0.931)
  Pallas kernels: 94 us -> 87.4 us
    pallas_call x1, Pallas kernels: 94 us -> 87.4 us  [local(): pl.pallas_call(functools.partial(kernel, n_dp, n_pipe), out_shape=jax.Sha...]
where the time goes in v3:
time: 88.8 us; the launch traced here: 88.7 us
  Pallas kernels  87.4 us (98%)
  local copies, waits for them, and re-layouts  1.26 us (1%)
    pallas_call x1, Pallas kernels, local(): pl.pallas_call(functools.partial(kernel, n_dp, n_pipe), out_shape=jax.Sha...  87.4 us

profile of v3, /device:TPU:1, one launch (start us, length us, event | category | flops | bytes accessed | tf_op | source)
XLA Modules:
  0.0 88.7 jit_solution(12230626473193752544)
XLA Ops:
  0.0 87.4 %influence.1 = f32[4,32]{1,0:T(4,128)} custom-call(bf16[1,512,8192]{2,1,0:T(8,128)(2,1)} %x_hbm.1, bf16[512,8192]{1,0:T(8,128)(2,1)} %cot_hbm.1, bf16[1,8192,512]{2,1,0:T(8,128)(2,1)} %d_hbm.1, bf16[1,512,8192]{2,1,0:T(8,128)(2,1)} %e_hbm.1, bf16[1,4,8192]{2,1,0:T(4,128)(2,1)} %v_ref.1, bf16[1,4,8192]{2,1,0:T(4,128)(2,1)} %i_ref.1, ...), custom_call_target="tpu_custom_call" | custom-call | tf_op jit(solution)/shard_map/influence/pallas_call | solution.py:662
  87.4 1.3 %copy.12 = f32[4,32]{1,0:T(4,128)} copy(f32[4,32]{1,0:T(4,128)} %influence.1) | data formatting | bytes 1024

commit v4 on v3

--- a/solution.py
+++ b/solution.py
@@ -29,13 +29,19 @@
     cot_hbm,
     d_hbm,
     e_hbm,
+    v_hbm,
+    i_hbm,
+    hc_hbm,
+    ic_hbm,
+    len_hbm,
+    qe_hbm,
+    out_ref,
     v_ref,
     i_ref,
     hc_ref,
     ic_ref,
     len_ref,
     qe_ref,
-    out_ref,
     x_v,
     cot_v,
     d_v,
@@ -55,6 +61,7 @@
     hp_acc,
     total,
     s_all,
+    load_small,
     load_e,
     load_d,
     load_cot,
@@ -78,6 +85,7 @@
     hp_recv,
     s_send,
     s_recv,
+    go_sem,
 ):
     lane = lax.axis_index("dp")
     layer = lax.axis_index("pipe")
@@ -94,7 +102,7 @@
     share = rank // n_dp
     wide = width // CHUNKS
     piece = width // PIECES
-    n_example = len_ref.shape[0]
+    n_example = len_ref.shape[1]
     sibling = {"pipe": layer + 1 - 2 * core}
     above = {"pipe": lax.rem(2 * chip + 2, n_pipe)}
 
@@ -130,25 +138,53 @@
         cols = pl.ds(pl.multiple_of(k * piece, piece), piece)
         return pltpu.make_async_copy(x_hbm.at[0, :, cols], x_v.at[k], load_x.at[k])
 
+    small = [
+        pltpu.make_async_copy(src, dst, load_small.at[n])
+        for n, (src, dst) in enumerate(
+            (
+                (ic_hbm, ic_ref),
+                (v_hbm, v_ref),
+                (i_hbm, i_ref),
+                (hc_hbm, hc_ref),
+                (len_hbm, len_ref),
+                (qe_hbm, qe_ref),
+            )
+        )
+    ]
+    for copy in small:
+        copy.start()
     for c in range(CHUNKS):
         load_expand(c).start()
-    for c in range(CHUNKS):
-        load_down(c).start()
-    for k in range(PIECES):
-        load_cotangent(k).start()
-    for k in range(PIECES):
-        load_activation(k).start()
 
     barrier = pltpu.get_barrier_semaphore()
+    last = n_pipe - 1
     for k in range(1, n_dp):
         pl.semaphore_signal(
             barrier, 1, device_id={"dp": lax.rem(lane + k, n_dp)}, device_id_type=MESH
         )
-    for k in range(1, n_pipe):
+    pl.semaphore_signal(barrier, 1, device_id=sibling, device_id_type=MESH)
+
+    @pl.when((core == 0) & (chip > 0))
+    def _():
         pl.semaphore_signal(
-            barrier, 1, device_id={"pipe": lax.rem(layer + k, n_pipe)}, device_id_type=MESH
-        )
-    pl.semaphore_wait(barrier, n_dp + n_pipe - 2)
+            barrier, 1, device_id={"pipe": jnp.maximum(layer - 1, 0)}, device_id_type=MESH
+        )
+
+    @pl.when(layer < last - 1)
+    def _():
+        pl.semaphore_signal(barrier, 1, device_id={"pipe": last}, device_id_type=MESH)
+
+    waits_above = jnp.where((core == 1) & (layer < last), 1, 0)
+    waits_column = jnp.where(layer == last, n_pipe - 2, 0)
+    pl.semaphore_wait(barrier, n_dp + waits_above + waits_column)
+
+    @pl.when(layer == last)
+    def _():
+        for target in range(last):
+            pl.semaphore_signal(go_sem, 1, device_id={"pipe": target}, device_id_type=MESH)
+
+    for copy in small:
+        copy.wait()
 
     v_rows = v_ref[0].astype(F32)
     rows_all[lane] = jnp.concatenate([v_rows, i_ref[0].astype(F32)], axis=0).astype(BF16)
@@ -239,6 +275,7 @@
 
     for c in range(CHUNKS):
         load_expand(c).wait()
+        load_down(c).start()
         born = v_wide[:, span(c)] + jnp.dot(ic_lane, e_v[:, span(c)], preferred_element_type=F32)
         sent[layer, :, span(c)] = born.astype(BF16)
 
@@ -250,12 +287,16 @@
         def _():
             part_copy(c).start()
 
-        @pl.when(is_upper & jnp.logical_not(pairs_up))
+        @pl.when(is_upper & jnp.logical_not(pairs_up) & jnp.logical_not(is_top))
         def _():
             up_copy(layer, 1, c).start()
 
     for c in range(CHUNKS):
         load_down(c).wait()
+    for k in range(PIECES):
+        load_cotangent(k).start()
+    for k in range(PIECES):
+        load_activation(k).start()
 
     def take(ref, u, n, c):
         return ref[pl.ds(u, n), :, span(c)].astype(F32).reshape(n * group, wide)
@@ -389,9 +430,14 @@
         token = lax.broadcasted_iota(jnp.int32, (every, tokens), 1)
         count = jnp.zeros((every, tokens), jnp.int32)
         for e in range(n_example):
-            count = jnp.where(token // SLOT == e, len_ref[e], count)
+            count = jnp.where(token // SLOT == e, len_ref[:, e : e + 1], count)
         live = jnp.where(lax.rem(token, SLOT) < count, 1.0, 0.0)
         hp_all[layer] = (hp_acc[...] * live).astype(BF16)
+
+        @pl.when(layer < last)
+        def _():
+            pl.semaphore_wait(go_sem, 1)
+
         for target in range(1, n_chip):
 
             @pl.when(chip < target)
@@ -657,14 +703,19 @@
         every = group * n_dp
         hbm = pl.BlockSpec(memory_space=pl.ANY)
         vmem = pl.BlockSpec(memory_space=pltpu.VMEM)
-        smem = pl.BlockSpec(memory_space=pltpu.SMEM)
         dma = pltpu.SemaphoreType.DMA
         return pl.pallas_call(
             functools.partial(kernel, n_dp, n_pipe),
             out_shape=jax.ShapeDtypeStruct((n_example, queries), F32),
-            in_specs=[hbm, hbm, hbm, hbm, vmem, vmem, vmem, vmem, smem, vmem],
+            in_specs=[hbm] * 10,
             out_specs=vmem,
             scratch_shapes=[
+                pltpu.VMEM(value.shape, BF16),
+                pltpu.VMEM(inputs.shape, BF16),
+                pltpu.VMEM(hidden_cols.shape, BF16),
+                pltpu.VMEM(inner_cols.shape, BF16),
+                pltpu.VMEM((1, n_example), jnp.int32),
+                pltpu.VMEM((1, queries), jnp.int32),
                 pltpu.VMEM((PIECES, tokens, width // PIECES), BF16),
                 pltpu.VMEM((PIECES, tokens, width // PIECES), BF16),
                 pltpu.VMEM((width, rank), BF16),
@@ -684,6 +735,7 @@
                 pltpu.VMEM((every, tokens), F32),
                 pltpu.VMEM((every, tokens), F32),
                 pltpu.VMEM((n_pipe, 8, 128), F32),
+                dma((6,)),
                 dma((CHUNKS,)),
                 dma((CHUNKS,)),
                 dma((PIECES,)),
@@ -707,6 +759,7 @@
                 dma((n_pipe,)),
                 dma((n_pipe,)),
                 dma,
+                pltpu.SemaphoreType.REGULAR,
             ],
             compiler_params=pltpu.CompilerParams(
                 collective_id=0, has_side_effects=True, vmem_limit_bytes=58 << 20
@@ -721,7 +774,7 @@
             inputs,
             hidden_cols,
             inner_cols,
-            lengths,
+            lengths.reshape(1, n_example),
             query.reshape(1, queries),
         )
 

time: 88.8 us -> 84.6 us (0.953)
  Pallas kernels: 87.4 us -> 83.2 us
    pallas_call x1, Pallas kernels: 87.4 us -> 83.2 us  [local(): pl.pallas_call(functools.partial(kernel, n_dp, n_pipe), out_shape=jax.Sha...]
where the time goes in v4:
time: 84.6 us; the launch traced here: 84.5 us
  Pallas kernels  83.2 us (98%)
  local copies, waits for them, and re-layouts  1.26 us (1%)
    pallas_call x1, Pallas kernels, local(): pl.pallas_call(functools.partial(kernel, n_dp, n_pipe), out_shape=jax.Sha...  83.2 us

profile of v4, /device:TPU:1, one launch (start us, length us, event | category | flops | bytes accessed | tf_op | source)
XLA Modules:
  0.0 84.5 jit_solution(17379152065274751855)
XLA Ops:
  0.0 83.2 %influence.1 = f32[4,32]{1,0:T(4,128)} custom-call(bf16[1,512,8192]{2,1,0:T(8,128)(2,1)} %x_hbm.1, bf16[512,8192]{1,0:T(8,128)(2,1)} %cot_hbm.1, bf16[1,8192,512]{2,1,0:T(8,128)(2,1)} %d_hbm.1, bf16[1,512,8192]{2,1,0:T(8,128)(2,1)} %e_hbm.1, bf16[1,4,8192]{2,1,0:T(4,128)(2,1)} %v_hbm.1, bf16[1,4,8192]{2,1,0:T(4,128)(2,1)} %i_hbm.1, ...), custom_call_target="tpu_custom_call" | custom-call | tf_op jit(solution)/shard_map/influence/pallas_call | solution.py:707
  83.2 1.3 %copy.12 = f32[4,32]{1,0:T(4,128)} copy(f32[4,32]{1,0:T(4,128)} %influence.1) | data formatting | bytes 1024

commit v5 on v4

--- a/solution.py
+++ b/solution.py
@@ -15,6 +15,7 @@
 CHUNKS = 4
 PIECES = 8
 ALONE = 1
+AHEAD = 3
 LOW = 3
 
 
@@ -198,7 +199,9 @@
                 rows_all.at[lane], rows_all.at[lane], rows_send, rows_recv, lane_at(k)
             ).start()
 
-    @pl.when(core == 0)
+    is_low = chip < LOW
+
+    @pl.when((core == 0) & jnp.logical_not(is_low))
     def _():
         spread_rows()
 
@@ -293,10 +296,16 @@
 
     for c in range(CHUNKS):
         load_down(c).wait()
-    for k in range(PIECES):
-        load_cotangent(k).start()
-    for k in range(PIECES):
-        load_activation(k).start()
+
+    def first_loads():
+        for k in range(AHEAD):
+            load_cotangent(k).start()
+        for k in range(AHEAD):
+            load_activation(k).start()
+
+    @pl.when(jnp.logical_not(is_low))
+    def _():
+        first_loads()
 
     def take(ref, u, n, c):
         return ref[pl.ds(u, n), :, span(c)].astype(F32).reshape(n * group, wide)
@@ -384,7 +393,10 @@
                 remote(k_all.at[lane], k_all.at[lane], k_send, k_recv, lane_at(k)).start()
 
         spread_factors(u, 1)
-        spread_rows()
+
+        @pl.when(jnp.logical_not(is_low))
+        def _():
+            spread_rows()
 
     def placed(first):
         row = lax.broadcasted_iota(jnp.int32, (every, queries), 0)
@@ -398,11 +410,21 @@
     ic_placed = jnp.dot(placed(half), ic_ref[0], preferred_element_type=F32).astype(BF16)
     def token_part(k):
         load_cotangent(k).wait()
+
+        @pl.when(k + AHEAD < PIECES)
+        def _():
+            load_cotangent(jnp.minimum(k + AHEAD, PIECES - 1)).start()
+
         cols = pl.ds(pl.multiple_of(k * piece, piece), piece)
         u_acc[...] += nt(e_v[:, cols], cot_v[k])
 
     def row_part(k):
         load_activation(k).wait()
+
+        @pl.when(k + AHEAD < PIECES)
+        def _():
+            load_activation(jnp.minimum(k + AHEAD, PIECES - 1)).start()
+
         cols = pl.ds(pl.multiple_of(k * piece, piece), piece)
         gathered = rows_all[:, :, cols].astype(F32).reshape(every, piece)
         of_value = lax.rem(lax.broadcasted_iota(jnp.int32, (every, piece), 0), group) < half
@@ -486,8 +508,6 @@
     hc_placed = jnp.dot(placed(0), hc_ref[0], preferred_element_type=F32).astype(BF16)
     ic_placed = jnp.dot(placed(half), ic_ref[0], preferred_element_type=F32).astype(BF16)
 
-    is_low = chip < LOW
-
     def token_end(step):
         late = jnp.where(step >= chip, PIECES, 0)
         return jnp.where(is_low, late, jnp.clip(4 + 2 * step, 0, PIECES))
@@ -498,6 +518,11 @@
 
     def token_side(step, before_token, before_row):
         end_token, end_row = token_end(step), row_end(step)
+
+        @pl.when(is_low & (before_token == 0) & (end_token > 0))
+        def _():
+            first_loads()
+            spread_rows()
 
         def token_step(k, carry):
             token_part(k)

time: 84.6 us -> 85.8 us (1.014)
  Pallas kernels: 83.2 us -> 84.4 us
    pallas_call x1, Pallas kernels: 83.2 us -> 84.4 us  [local(): pl.pallas_call(functools.partial(kernel, n_dp, n_pipe), out_shape=jax.Sha...]
where the time goes in v5:
time: 85.8 us; the launch traced here: 85.6 us
  Pallas kernels  84.4 us (98%)
  local copies, waits for them, and re-layouts  1.26 us (1%)
    pallas_call x1, Pallas kernels, local(): pl.pallas_call(functools.partial(kernel, n_dp, n_pipe), out_shape=jax.Sha...  84.4 us

profile of v5, /device:TPU:1, one launch (start us, length us, event | category | flops | bytes accessed | tf_op | source)
XLA Modules:
  0.0 85.6 jit_solution(17803938978323617719)
XLA Ops:
  0.0 84.4 %influence.1 = f32[4,32]{1,0:T(4,128)} custom-call(bf16[1,512,8192]{2,1,0:T(8,128)(2,1)} %x_hbm.1, bf16[512,8192]{1,0:T(8,128)(2,1)} %cot_hbm.1, bf16[1,8192,512]{2,1,0:T(8,128)(2,1)} %d_hbm.1, bf16[1,512,8192]{2,1,0:T(8,128)(2,1)} %e_hbm.1, bf16[1,4,8192]{2,1,0:T(4,128)(2,1)} %v_hbm.1, bf16[1,4,8192]{2,1,0:T(4,128)(2,1)} %i_hbm.1, ...), custom_call_target="tpu_custom_call" | custom-call | tf_op jit(solution)/shard_map/influence/pallas_call | solution.py:732
  84.4 1.3 %copy.12 = f32[4,32]{1,0:T(4,128)} copy(f32[4,32]{1,0:T(4,128)} %influence.1) | data formatting | bytes 1024

commit v6 on v4

--- a/solution.py
+++ b/solution.py
@@ -153,8 +153,18 @@
     ]
     for copy in small:
         copy.start()
-    for c in range(CHUNKS):
-        load_expand(c).start()
+    is_lower = core == 0
+    is_upper = core == 1
+
+    @pl.when(is_lower)
+    def _():
+        for c in range(CHUNKS):
+            load_expand(c).start()
+
+    @pl.when(is_upper)
+    def _():
+        for c in range(CHUNKS):
+            load_down(c).start()
 
     barrier = pltpu.get_barrier_semaphore()
     last = n_pipe - 1
@@ -197,10 +207,6 @@
             remote(
                 rows_all.at[lane], rows_all.at[lane], rows_send, rows_recv, lane_at(k)
             ).start()
-
-    @pl.when(core == 0)
-    def _():
-        spread_rows()
 
     row = lax.broadcasted_iota(jnp.int32, (group, queries), 0)
     col = lax.broadcasted_iota(jnp.int32, (group, queries), 1)
@@ -260,43 +266,38 @@
 
     others = pl.ds(0, n_dp - 1)
 
-    def part_copy(c):
+    def part_copy():
         return remote(
-            e_v.at[pl.ds(pl.multiple_of(lane * share, share), share), span(c)],
-            k_part.at[:, span(c)],
-            part_send.at[c],
-            part_recv.at[c],
+            e_hbm.at[0, pl.ds(pl.multiple_of(lane * share, share), share), :],
+            k_part,
+            part_send,
+            part_recv,
             sibling,
         )
 
-    is_lower = core == 0
-    is_upper = core == 1
     pairs_up = chip >= ALONE
 
-    for c in range(CHUNKS):
-        load_expand(c).wait()
-        load_down(c).start()
-        born = v_wide[:, span(c)] + jnp.dot(ic_lane, e_v[:, span(c)], preferred_element_type=F32)
-        sent[layer, :, span(c)] = born.astype(BF16)
-
-        @pl.when(is_lower)
-        def _():
+    @pl.when(is_lower & (chip > 0))
+    def _():
+        part_copy().start()
+
+    @pl.when(is_lower)
+    def _():
+        spread_rows()
+
+    def born(c):
+        own = v_wide[:, span(c)] + jnp.dot(ic_lane, e_v[:, span(c)], preferred_element_type=F32)
+        sent[layer, :, span(c)] = own.astype(BF16)
+
+    @pl.when(is_lower)
+    def _():
+        for c in range(CHUNKS):
+            load_expand(c).wait()
+            load_down(c).start()
+            born(c)
             own_copy(c).start()
-
-        @pl.when(is_lower & (chip > 0))
-        def _():
-            part_copy(c).start()
-
-        @pl.when(is_upper & jnp.logical_not(pairs_up) & jnp.logical_not(is_top))
-        def _():
-            up_copy(layer, 1, c).start()
-
-    for c in range(CHUNKS):
-        load_down(c).wait()
-    for k in range(PIECES):
-        load_cotangent(k).start()
-    for k in range(PIECES):
-        load_activation(k).start()
+        for c in range(CHUNKS):
+            load_down(c).wait()
 
     def take(ref, u, n, c):
         return ref[pl.ds(u, n), :, span(c)].astype(F32).reshape(n * group, wide)
@@ -332,12 +333,17 @@
 
         spread_factors(u, n)
 
-    def upper_stage(u, n):
+    def upper_stage(u, n, first):
         projected = jnp.zeros((n * group, rank), F32)
         for c in range(CHUNKS):
             pass_copy(u, n, c).wait_recv()
             projected += down(take(z_in, u, n, c), c)
         factor_copy(u, n).wait_recv()
+
+        @pl.when(first)
+        def _():
+            landed(k_all.at[others], k_recv)
+
         below = f_in[pl.ds(u, n)].astype(F32).reshape(n * group, rank).astype(BF16)
         projected += jnp.dot(below, k_all[...].reshape(rank, rank), preferred_element_type=F32)
         factor = keep(u, n, projected)
@@ -354,15 +360,36 @@
     @pl.when(is_upper)
     def _():
         u = layer - 1
+
+        @pl.when(chip > 0)
+        def _():
+            landed(k_part, part_recv)
+            coupled = jnp.zeros((share, rank), F32)
+            for c in range(CHUNKS):
+                load_down(c).wait()
+                load_expand(c).start()
+                coupled += jnp.dot(k_part[:, span(c)], d_v[span(c), :], preferred_element_type=F32)
+            k_all[lane] = coupled.astype(BF16)
+            for k in range(1, n_dp):
+                remote(k_all.at[lane], k_all.at[lane], k_send, k_recv, lane_at(k)).start()
+
+        @pl.when(chip == 0)
+        def _():
+            for c in range(CHUNKS):
+                load_down(c).wait()
+                load_expand(c).start()
+
         projected = jnp.zeros((group, rank), F32)
         for c in range(CHUNKS):
             landed(z_in.at[u, :, span(c)], z_recv.at[u, c])
             projected += down(take(z_in, u, 1, c), c)
         factor = keep(u, 1, projected)
-
-        @pl.when(jnp.logical_not(is_top))
-        def _():
-            for c in range(CHUNKS):
+        for c in range(CHUNKS):
+            load_expand(c).wait()
+
+            @pl.when(jnp.logical_not(is_top))
+            def _():
+                born(c)
                 put(u, 1, c, take(z_in, u, 1, c) + up(factor, c))
 
                 @pl.when(pairs_up)
@@ -371,20 +398,16 @@
 
                 @pl.when(jnp.logical_not(pairs_up))
                 def _():
+                    up_copy(layer, 1, c).start()
                     up_copy(u, 1, c).start()
-
-        @pl.when(chip > 0)
-        def _():
-            coupled = jnp.zeros((share, rank), F32)
-            for c in range(CHUNKS):
-                landed(k_part.at[:, span(c)], part_recv.at[c])
-                coupled += jnp.dot(k_part[:, span(c)], d_v[span(c), :], preferred_element_type=F32)
-            k_all[lane] = coupled.astype(BF16)
-            for k in range(1, n_dp):
-                remote(k_all.at[lane], k_all.at[lane], k_send, k_recv, lane_at(k)).start()
 
         spread_factors(u, 1)
         spread_rows()
+
+    for k in range(PIECES):
+        load_cotangent(k).start()
+    for k in range(PIECES):
+        load_activation(k).start()
 
     def placed(first):
         row = lax.broadcasted_iota(jnp.int32, (every, queries), 0)
@@ -519,14 +542,14 @@
         def _():
             settle()
 
-    def stage(u, n):
+    def stage(u, n, first):
         @pl.when(is_lower)
         def _():
             lower_stage(u, n)
 
         @pl.when(is_upper)
         def _():
-            upper_stage(u, n)
+            upper_stage(u, n, first)
 
     def collect_down(first, last):
         def body(i, carry):
@@ -542,18 +565,14 @@
         def _():
             below = jnp.maximum(chip - step, 0)
 
-            @pl.when((step == 1) & is_upper)
-            def _():
-                landed(k_all.at[others], k_recv)
-
             @pl.when(below >= ALONE)
             def _():
-                stage(2 * below, 2)
+                stage(2 * below, 2, step == 1)
 
             @pl.when(below < ALONE)
             def _():
                 def one(i, carry):
-                    stage(2 * below + 1 - i, 1)
+                    stage(2 * below + 1 - i, 1, (step == 1) & (i == 0))
                     return carry
 
                 lax.fori_loop(0, 2, one, 0)
@@ -645,8 +664,7 @@
 
     @pl.when(is_lower & (chip > 0))
     def _():
-        for c in range(CHUNKS):
-            part_copy(c).wait_send()
+        part_copy().wait_send()
 
     @pl.when(is_upper)
     def _():
@@ -748,8 +766,8 @@
                 dma((n_pipe, CHUNKS)),
                 dma((n_pipe,)),
                 dma((n_pipe,)),
-                dma((CHUNKS,)),
-                dma((CHUNKS,)),
+                dma,
+                dma,
                 dma,
                 dma,
                 dma((n_pipe,)),

time: 84.6 us -> 83.6 us (0.988)
  Pallas kernels: 83.2 us -> 82.2 us
    pallas_call x1, Pallas kernels: 83.2 us -> 82.2 us  [local(): pl.pallas_call(functools.partial(kernel, n_dp, n_pipe), out_shape=jax.Sha...]
where the time goes in v6:
time: 83.6 us; the launch traced here: 83.4 us
  Pallas kernels  82.2 us (98%)
  local copies, waits for them, and re-layouts  1.26 us (2%)
    pallas_call x1, Pallas kernels, local(): pl.pallas_call(functools.partial(kernel, n_dp, n_pipe), out_shape=jax.Sha...  82.2 us

profile of v6, /device:TPU:1, one launch (start us, length us, event | category | flops | bytes accessed | tf_op | source)
XLA Modules:
  0.0 83.4 jit_solution(6712590429789430644)
XLA Ops:
  0.0 82.2 %influence.1 = f32[4,32]{1,0:T(4,128)} custom-call(bf16[1,512,8192]{2,1,0:T(8,128)(2,1)} %x_hbm.1, bf16[512,8192]{1,0:T(8,128)(2,1)} %cot_hbm.1, bf16[1,8192,512]{2,1,0:T(8,128)(2,1)} %d_hbm.1, bf16[1,512,8192]{2,1,0:T(8,128)(2,1)} %e_hbm.1, bf16[1,4,8192]{2,1,0:T(4,128)(2,1)} %v_hbm.1, bf16[1,4,8192]{2,1,0:T(4,128)(2,1)} %i_hbm.1, ...), custom_call_target="tpu_custom_call" | custom-call | tf_op jit(solution)/shard_map/influence/pallas_call | solution.py:725
  82.2 1.3 %copy.12 = f32[4,32]{1,0:T(4,128)} copy(f32[4,32]{1,0:T(4,128)} %influence.1) | data formatting | bytes 1024

commit v7 on v6

--- a/solution.py
+++ b/solution.py
@@ -513,11 +513,11 @@
 
     def token_end(step):
         late = jnp.where(step >= chip, PIECES, 0)
-        return jnp.where(is_low, late, jnp.clip(4 + 2 * step, 0, PIECES))
+        return jnp.where(is_low, late, jnp.clip(4 + 4 * step, 0, PIECES))
 
     def row_end(step):
         late = jnp.where(step >= chip, PIECES, 0)
-        return jnp.where(is_low, late, jnp.clip(2 * step - 2, 0, PIECES))
+        return jnp.where(is_low, late, jnp.clip(3 * step - 3, 0, PIECES))
 
     def token_side(step, before_token, before_row):
         end_token, end_row = token_end(step), row_end(step)
@@ -558,7 +558,7 @@
 
         lax.fori_loop(0, jnp.maximum(first - last + 1, 0), body, 0)
 
-    early = 2
+    early = 4
 
     def advance(step, carry):
         @pl.when((step >= 1) & (step <= chip))
@@ -581,7 +581,7 @@
         before_row = jnp.where(step == 0, 0, row_end(step - 1))
         token_side(step, before_token, before_row)
 
-        @pl.when((step == n_chip - 2) & is_top)
+        @pl.when((step == n_chip - 3) & is_top)
         def _():
             collect_down(n_chip - 2, early)
 

time: 83.6 us -> 81.4 us (0.974)
  Pallas kernels: 82.2 us -> 80 us
    pallas_call x1, Pallas kernels: 82.2 us -> 80 us  [local(): pl.pallas_call(functools.partial(kernel, n_dp, n_pipe), out_shape=jax.Sha...]
where the time goes in v7:
time: 81.4 us; the launch traced here: 81.2 us
  Pallas kernels  80 us (98%)
  local copies, waits for them, and re-layouts  1.26 us (2%)
    pallas_call x1, Pallas kernels, local(): pl.pallas_call(functools.partial(kernel, n_dp, n_pipe), out_shape=jax.Sha...  80 us

profile of v7, /device:TPU:1, one launch (start us, length us, event | category | flops | bytes accessed | tf_op | source)
XLA Modules:
  0.0 81.2 jit_solution(3492453296464911577)
XLA Ops:
  0.0 80.0 %influence.1 = f32[4,32]{1,0:T(4,128)} custom-call(bf16[1,512,8192]{2,1,0:T(8,128)(2,1)} %x_hbm.1, bf16[512,8192]{1,0:T(8,128)(2,1)} %cot_hbm.1, bf16[1,8192,512]{2,1,0:T(8,128)(2,1)} %d_hbm.1, bf16[1,512,8192]{2,1,0:T(8,128)(2,1)} %e_hbm.1, bf16[1,4,8192]{2,1,0:T(4,128)(2,1)} %v_hbm.1, bf16[1,4,8192]{2,1,0:T(4,128)(2,1)} %i_hbm.1, ...), custom_call_target="tpu_custom_call" | custom-call | tf_op jit(solution)/shard_map/influence/pallas_call | solution.py:725
  80.0 1.3 %copy.12 = f32[4,32]{1,0:T(4,128)} copy(f32[4,32]{1,0:T(4,128)} %influence.1) | data formatting | bytes 1024

commit v8 on v7

--- a/solution.py
+++ b/solution.py
@@ -281,9 +281,7 @@
     def _():
         part_copy().start()
 
-    @pl.when(is_lower)
-    def _():
-        spread_rows()
+    is_low = chip < LOW
 
     def born(c):
         own = v_wide[:, span(c)] + jnp.dot(ic_lane, e_v[:, span(c)], preferred_element_type=F32)
@@ -298,6 +296,10 @@
             own_copy(c).start()
         for c in range(CHUNKS):
             load_down(c).wait()
+
+        @pl.when(jnp.logical_not(is_low))
+        def _():
+            spread_rows()
 
     def take(ref, u, n, c):
         return ref[pl.ds(u, n), :, span(c)].astype(F32).reshape(n * group, wide)
@@ -402,7 +404,10 @@
                     up_copy(u, 1, c).start()
 
         spread_factors(u, 1)
-        spread_rows()
+
+        @pl.when(jnp.logical_not(is_low))
+        def _():
+            spread_rows()
 
     for k in range(PIECES):
         load_cotangent(k).start()
@@ -509,8 +514,6 @@
     hc_placed = jnp.dot(placed(0), hc_ref[0], preferred_element_type=F32).astype(BF16)
     ic_placed = jnp.dot(placed(half), ic_ref[0], preferred_element_type=F32).astype(BF16)
 
-    is_low = chip < LOW
-
     def token_end(step):
         late = jnp.where(step >= chip, PIECES, 0)
         return jnp.where(is_low, late, jnp.clip(4 + 4 * step, 0, PIECES))
@@ -521,6 +524,10 @@
 
     def token_side(step, before_token, before_row):
         end_token, end_row = token_end(step), row_end(step)
+
+        @pl.when(is_low & (before_token == 0) & (end_token > 0))
+        def _():
+            spread_rows()
 
         def token_step(k, carry):
             token_part(k)

time: 81.4 us -> 83.2 us (1.022)
  Pallas kernels: 80 us -> 81.8 us
    pallas_call x1, Pallas kernels: 80 us -> 81.8 us  [local(): pl.pallas_call(functools.partial(kernel, n_dp, n_pipe), out_shape=jax.Sha...]
where the time goes in v8:
time: 83.2 us; the launch traced here: 83.1 us
  Pallas kernels  81.8 us (98%)
  local copies, waits for them, and re-layouts  1.26 us (2%)
    pallas_call x1, Pallas kernels, local(): pl.pallas_call(functools.partial(kernel, n_dp, n_pipe), out_shape=jax.Sha...  81.8 us

profile of v8, /device:TPU:1, one launch (start us, length us, event | category | flops | bytes accessed | tf_op | source)
XLA Modules:
  0.0 83.1 jit_solution(16677537344949871063)
XLA Ops:
  0.0 81.8 %influence.1 = f32[4,32]{1,0:T(4,128)} custom-call(bf16[1,512,8192]{2,1,0:T(8,128)(2,1)} %x_hbm.1, bf16[512,8192]{1,0:T(8,128)(2,1)} %cot_hbm.1, bf16[1,8192,512]{2,1,0:T(8,128)(2,1)} %d_hbm.1, bf16[1,512,8192]{2,1,0:T(8,128)(2,1)} %e_hbm.1, bf16[1,4,8192]{2,1,0:T(4,128)(2,1)} %v_hbm.1, bf16[1,4,8192]{2,1,0:T(4,128)(2,1)} %i_hbm.1, ...), custom_call_target="tpu_custom_call" | custom-call | tf_op jit(solution)/shard_map/influence/pallas_call | solution.py:732
  81.8 1.3 %copy.12 = f32[4,32]{1,0:T(4,128)} copy(f32[4,32]{1,0:T(4,128)} %influence.1) | data formatting | bytes 1024

commit v9 on v7

--- a/solution.py
+++ b/solution.py
@@ -281,10 +281,6 @@
     def _():
         part_copy().start()
 
-    @pl.when(is_lower)
-    def _():
-        spread_rows()
-
     def born(c):
         own = v_wide[:, span(c)] + jnp.dot(ic_lane, e_v[:, span(c)], preferred_element_type=F32)
         sent[layer, :, span(c)] = own.astype(BF16)
@@ -296,6 +292,7 @@
             load_down(c).start()
             born(c)
             own_copy(c).start()
+        spread_rows()
         for c in range(CHUNKS):
             load_down(c).wait()
 

time: 81.4 us -> 81.5 us (level)
  no operation moved by 1% of the time
where the time goes in v9:
time: 81.5 us; the launch traced here: 81.3 us
  Pallas kernels  80.1 us (98%)
  local copies, waits for them, and re-layouts  1.26 us (2%)
    pallas_call x1, Pallas kernels, local(): pl.pallas_call(functools.partial(kernel, n_dp, n_pipe), out_shape=jax.Sha...  80.1 us

profile of v9, /device:TPU:1, one launch (start us, length us, event | category | flops | bytes accessed | tf_op | source)
XLA Modules:
  0.0 81.3 jit_solution(2289530668576324056)
XLA Ops:
  0.0 80.1 %influence.1 = f32[4,32]{1,0:T(4,128)} custom-call(bf16[1,512,8192]{2,1,0:T(8,128)(2,1)} %x_hbm.1, bf16[512,8192]{1,0:T(8,128)(2,1)} %cot_hbm.1, bf16[1,8192,512]{2,1,0:T(8,128)(2,1)} %d_hbm.1, bf16[1,512,8192]{2,1,0:T(8,128)(2,1)} %e_hbm.1, bf16[1,4,8192]{2,1,0:T(4,128)(2,1)} %v_hbm.1, bf16[1,4,8192]{2,1,0:T(4,128)(2,1)} %i_hbm.1, ...), custom_call_target="tpu_custom_call" | custom-call | tf_op jit(solution)/shard_map/influence/pallas_call | solution.py:722
  80.1 1.3 %copy.12 = f32[4,32]{1,0:T(4,128)} copy(f32[4,32]{1,0:T(4,128)} %influence.1) | data formatting | bytes 1024
